TPU v7x, 32 devices: a whole 2x2x4 slice. The times are simulated.
32 devices in a mesh: group: 2 (over x), lat: 16 (over z, y, core).
Axes of the slice: x: 2, y: 2, z: 4, core: 2. Of those that a mesh axis runs over, the one named last changes fastest.
Arguments:
- field: bfloat16 [1024, 512, 512], P(('group', 'lat')), parts along dimension 0, may hold values from -6 to 6
- lat_modes: float32 [64, 16, 16], replicated, may hold values from -1.5 to 1.5
- lat_gains: float32 [64, 16], replicated, may hold values from 2 to 16
- lat_local: float32 [16, 16], replicated, may hold values from -1.5 to 1.5
- depth_modes: float32 [16, 16, 16], replicated, may hold values from -1.5 to 1.5
- depth_local: float32 [16, 16], replicated, may hold values from -1.5 to 1.5
Outputs:
- result: bfloat16 [1024, 512, 512], P(('group', 'lat')), parts along dimension 0
There are 2 independent parts, one for each index of `group`. A program takes and returns all parts, laid end to end along the dimension named above; an argument that names none is the same for every part. Nothing has to cross between parts.
All inputs are finite; a program needn't handle non-finite values.
Results may differ from a plain program's by a relative error of at most 0.001.
Values may be sent and summed in bfloat16 or wider, within the bound.
A program may use at most 192 MiB of HBM per device.

v0:
```python
import functools
import math

import jax
import jax.numpy as jnp
import numpy as np
from jax import lax
from jax.experimental import pallas as pl
from jax.experimental.pallas import tpu as pltpu
from jax.sharding import PartitionSpec as P

LINK = jnp.float16
SCALE_OUT = 256.0
SCALE_BACK = 1.0 / 16.0
K0 = math.sqrt(2.0 / math.pi)
K1 = K0 * 0.044715
MIB = 1 << 20


def cosine_basis(length, modes):
    order = np.arange(modes, dtype=np.float64)[:, None]
    place = np.arange(length, dtype=np.float64)[None, :]
    scales = np.where(order == 0.0, math.sqrt(1.0 / length), math.sqrt(2.0 / length))
    return (np.cos(math.pi * order * (place + 0.5) / length) * scales).astype(np.float32)


def halves(x):
    high = jnp.asarray(x).astype(jnp.bfloat16)
    low = (x - high.astype(jnp.float32)).astype(jnp.bfloat16)
    return high, low


def outer_halves(x):
    high = lax.reduce_precision(x, 8, 7)
    return high.astype(jnp.bfloat16), (x - high).astype(jnp.bfloat16)


def np_halves(x):
    high = np.asarray(x, dtype=jnp.bfloat16)
    low = np.asarray(x - high.astype(np.float32), dtype=jnp.bfloat16)
    return high, low


def dot(a, b):
    return jnp.dot(a, b, preferred_element_type=jnp.float32)


def gelu(x):
    half = 0.5 * x
    return half + half * jnp.tanh(x * (K0 + K1 * (x * x)))


def forward_kernel(basis_ref, u_ref, out_ref):
    modes = out_ref.shape[1]

    def body(row, carry):
        both = dot(basis_ref[...], u_ref[row])
        out_ref[row] = (both[:modes] + both[modes:]) * SCALE_OUT
        return carry

    lax.fori_loop(0, u_ref.shape[0], body, 0)


def forward(field, basis, start, rows):
    _, width, cells = field.shape
    modes = basis.shape[0] // 2
    step = math.gcd(rows, 4)
    return pl.pallas_call(
        forward_kernel,
        grid=(rows // step,),
        in_specs=[
            pl.BlockSpec(basis.shape, lambda i: (0, 0)),
            pl.BlockSpec((step, width, cells), lambda i: (i + start // step, 0, 0)),
        ],
        out_specs=pl.BlockSpec((step, modes, cells), lambda i: (i, 0, 0)),
        out_shape=jax.ShapeDtypeStruct((rows, modes, cells), jnp.float32),
        compiler_params=pltpu.CompilerParams(vmem_limit_bytes=40 * MIB),
        cost_estimate=pl.CostEstimate(
            flops=4 * rows * modes * width * cells,
            bytes_accessed=rows * cells * (2 * width + 4 * modes),
            transcendentals=0,
        ),
    )(basis, field)


def middle_kernel(chunks, chans, *refs):
    g_refs = refs[:chunks]
    f_refs = refs[chunks : 2 * chunks]
    b_refs = refs[2 * chunks : 3 * chunks]
    gain_ref, diag_ref = refs[3 * chunks : 3 * chunks + 2]
    out_refs = refs[3 * chunks + 2 :]
    modes = diag_ref.shape[1]
    coef = None
    for g_ref, f_ref in zip(g_refs, f_refs):
        high, low = halves(g_ref[0])
        both = dot(f_ref[...], high)
        part = both[:modes] + both[modes:] + dot(f_ref[:modes], low)
        coef = part if coef is None else coef + part
    coef = coef * gain_ref[0]
    tiles = []
    for lane in range(0, coef.shape[1], 128):
        tile = coef[:, lane : lane + 128]
        total = tile * diag_ref[chans - 1]
        for at in range(2 * chans - 1):
            shift = at - (chans - 1)
            if shift != 0:
                total += pltpu.roll(tile, (-shift) % 128, 1) * diag_ref[at]
        tiles.append(total)
    mixed = jnp.concatenate(tiles, axis=1) if len(tiles) > 1 else tiles[0]
    high, low = halves(mixed)
    stacked = jnp.concatenate([high, low, high], axis=0)
    for b_ref, out_ref in zip(b_refs, out_refs):
        out_ref[0] = dot(b_ref[...], stacked)


def middle(gathered, fronts, backs, gains, diags):
    chunks = len(gathered)
    count, length, width = gathered[0].shape
    modes = diags.shape[1]
    chans = (diags.shape[0] + 1) // 2
    whole = lambda a: pl.BlockSpec(a.shape, lambda i: (0,) * a.ndim)
    block = pl.BlockSpec((1, length, width), lambda i: (i, 0, 0))
    return pl.pallas_call(
        functools.partial(middle_kernel, chunks, chans),
        grid=(count,),
        in_specs=[block] * chunks
        + [whole(a) for a in fronts]
        + [whole(a) for a in backs]
        + [pl.BlockSpec((1, 1, width), lambda i: (i, 0, 0)), whole(diags)],
        out_specs=[block] * chunks,
        out_shape=[jax.ShapeDtypeStruct((count, length, width), jnp.float32)] * chunks,
        compiler_params=pltpu.CompilerParams(vmem_limit_bytes=40 * MIB),
    )(*gathered, *fronts, *backs, gains, diags)


def tail_kernel(piece, u_ref, back_ref, basis_ref, local_ref, depth_ref, *refs):
    out_ref = refs[-1]
    _, width, cells = u_ref.shape
    block = local_ref.shape[1]
    high, low = halves(back_ref[0])
    stacked = jnp.concatenate([high, low, high], axis=0)

    def body(at, carry):
        rows = pl.ds(pl.multiple_of(at * piece, piece), piece)
        u = u_ref[0, rows, :]
        spect = dot(basis_ref[rows, :], stacked)
        parts = []
        for lane in range(0, cells, block):
            tile = u[:, lane : lane + block]
            parts.append(dot(tile, local_ref[0]) + dot(tile, local_ref[1]))
        local = jnp.concatenate(parts, axis=1) if len(parts) > 1 else parts[0]
        first = u.astype(jnp.float32) + gelu(spect + local)
        high1, low1 = halves(first)
        mix = dot(high1, depth_ref[0]) + dot(low1, depth_ref[0]) + dot(high1, depth_ref[1])
        out_ref[0, rows, :] = (first + gelu(mix)).astype(out_ref.dtype)
        return carry

    lax.fori_loop(0, width // piece, body, 0)


def tail(field, back, basis, local, depth, previous, start):
    rows, modes, cells = back.shape
    width = field.shape[1]
    whole = lambda a: pl.BlockSpec(a.shape, lambda i: (0,) * a.ndim)
    operands = [field, back, basis, local, depth]
    specs = [
        pl.BlockSpec((1, width, cells), lambda i: (i + start, 0, 0)),
        pl.BlockSpec((1, modes, cells), lambda i: (i, 0, 0)),
        whole(basis),
        whole(local),
        whole(depth),
    ]
    aliases = {}
    if previous is not None:
        aliases = {len(operands): 0}
        operands.append(previous)
        specs.append(pl.BlockSpec(memory_space=pl.ANY))
    return pl.pallas_call(
        functools.partial(tail_kernel, math.gcd(width, 256)),
        grid=(rows,),
        in_specs=specs,
        out_specs=pl.BlockSpec((1, width, cells), lambda i: (i + start, 0, 0)),
        out_shape=jax.ShapeDtypeStruct(field.shape, jnp.bfloat16),
        input_output_aliases=aliases,
        compiler_params=pltpu.CompilerParams(vmem_limit_bytes=48 * MIB),
        cost_estimate=pl.CostEstimate(
            flops=2 * rows * width * cells * (4 * cells),
            bytes_accessed=4 * rows * width * cells,
            transcendentals=2 * rows * width * cells,
        ),
    )(*operands)


def block_diagonal(small, size):
    chans = small.shape[0]
    copies = size // chans
    ids = np.arange(size) // chans
    mask = (ids[:, None] == ids[None, :]).astype(np.float32)
    return jnp.tile(small, (copies, copies)) * mask


def shards(field, lat_modes, lat_gains, lat_local, depth_modes, depth_local):
    highest = lax.Precision.HIGHEST
    devices = lax.axis_size("lat")
    rows_dev, width_y, cells = field.shape
    modes_x, chans, _ = lat_modes.shape
    modes_y = lat_gains.shape[0]
    modes_z = depth_modes.shape[0]
    depth = cells // chans
    width_x = rows_dev * devices
    chunks = 2 if rows_dev % 16 == 0 else 1
    rows = rows_dev // chunks
    splits = max(1, devices // modes_y)
    held = modes_y * splits // devices
    span = cells // splits
    basis_x = cosine_basis(width_x, modes_x)
    basis_y = cosine_basis(width_y, modes_y)
    basis_z = cosine_basis(depth, modes_z)

    high_y, low_y = np_halves(basis_y)
    front_y = jnp.asarray(np.concatenate([high_y, low_y], axis=0))
    back_y = jnp.asarray(np.concatenate([high_y, high_y, low_y], axis=0).T.copy())
    fronts, backs = [], []
    for chunk in range(chunks):
        part = basis_x.reshape(modes_x, devices, chunks, rows)[:, :, chunk].reshape(modes_x, -1)
        high_x, low_x = np_halves(part)
        fronts.append(jnp.asarray(np.concatenate([high_x, low_x], axis=0)))
        backs.append(jnp.asarray(np.concatenate([high_x, high_x, low_x], axis=0).T.copy()))

    gathered = []
    for chunk in range(chunks):
        coef_y = forward(field, front_y, chunk * rows, rows)
        sent = coef_y.astype(LINK).reshape(rows, modes_y, splits, span)
        sent = sent.transpose(1, 2, 0, 3).reshape(modes_y * splits, rows, span)
        gathered.append(lax.all_to_all(sent, "lat", split_axis=0, concat_axis=0, tiled=True))

    shift = np.arange(2 * chans - 1)[:, None, None] - (chans - 1)
    places = np.arange(chans)
    pick = (places[None, :, None] == places[None, None, :] + shift).astype(np.float32)
    diags = jnp.sum(lat_modes[None] * pick[:, None], axis=2)
    diags = jnp.tile(diags, (1, 1, 128 // chans))
    me = lax.axis_index("lat")
    gain_rows = lax.dynamic_slice_in_dim(lat_gains, me * held // splits, held, 0)
    gain_rows = jnp.tile(gain_rows * (SCALE_BACK / SCALE_OUT), (1, span // chans))[:, None, :]

    spread = np.kron(basis_z.T, np.eye(chans, dtype=np.float32))
    ids = np.arange(modes_z * chans) // chans
    mask = (ids[:, None] == ids[None, :]).astype(np.float32)
    mixers = jnp.tile(depth_modes.reshape(modes_z * chans, chans), (1, modes_z)) * mask
    inner = jnp.dot(mixers, spread.T, precision=highest)
    whole = jnp.dot(spread, inner, precision=highest) + block_diagonal(depth_local, cells)
    depth_pair = jnp.stack(outer_halves(whole))
    local_pair = jnp.stack(outer_halves(block_diagonal(lat_local, math.gcd(cells, 256))))

    received = []
    for got in gathered:
        got = got.reshape(devices, held, rows, span).transpose(1, 0, 2, 3).astype(jnp.float32)
        received.append(got.reshape(held, devices * rows, span))
    mixed = middle(received, fronts, backs, gain_rows, diags)
    returned = []
    for part in mixed:
        part = part.astype(LINK).reshape(held, devices, rows, span).transpose(1, 0, 2, 3)
        part = part.reshape(devices * held, rows, span)
        returned.append(lax.all_to_all(part, "lat", split_axis=0, concat_axis=0, tiled=True))
    out = None
    for chunk, part in enumerate(returned):
        part = part.reshape(modes_y, splits, rows, span).transpose(2, 0, 1, 3)
        part = part.reshape(rows, modes_y, cells).astype(jnp.float32) * (1.0 / SCALE_BACK)
        out = tail(field, part, back_y, local_pair, depth_pair, out, chunk * rows)
    return out


def solution(mesh):
    placed = (P(("group", "lat"), None, None), P(), P(), P(), P(), P())
    return jax.shard_map(
        shards,
        mesh=mesh,
        in_specs=placed,
        out_specs=P(("group", "lat"), None, None),
        check_vma=False,
    )
```

profile of v0, /device:TPU:0, one launch (start us, length us, event | category | flops | bytes accessed | tf_op | source)
XLA Modules:
  0.0 195.8 jit_solution(445326577981977641)
XLA Ops:
  0.0 0.9 copy-done.4
  0.9 6.2 %shard_map.173 = f32[16,64,512]{2,1,0:T(8,128)S(1)} custom-call(bf16[128,512]{1,0:T(8,128)(2,1)S(1)} %copy-done.4, bf16[32,512,512]{2,1,0:T(8,128)(2,1)} %u_ref.7), custom_call_target="tpu_custom_call" | custom-call | flops 1073741824 | bytes 10485760 | tf_op jit(solution)/shard_map/pallas_call | solution.py:68
  7.4 1.7 copy.62
  9.1 7.4 %all-to-all-start.1 = ((f16[64,16,512]{2,1,0:T(8,128)(2,1)}), f16[64,16,512]{2,1,0:T(8,128)(2,1)S(1)}, u32[]{:S(2)}, u32[]{:S(2)}) async-start(f16[64,16,512]{2,1,0:T(8,128)(2,1)} %copy.62), calls=%async_computation.1 | async-start | bytes 2097152 | tf_op jit(solution)/shard_map/all_to_all | solution.py:235
  16.5 6.2 %shard_map.172 = f32[16,64,512]{2,1,0:T(8,128)S(1)} custom-call(bf16[128,512]{1,0:T(8,128)(2,1)S(1)} %copy-done.5, bf16[32,512,512]{2,1,0:T(8,128)(2,1)} %u_ref.7), custom_call_target="tpu_custom_call" | custom-call | flops 1073741824 | bytes 10485760 | tf_op jit(solution)/shard_map/pallas_call | solution.py:68
  23.0 1.7 copy.60
  24.7 14.8 %all-to-all-done.1 = f16[64,16,512]{2,1,0:T(8,128)(2,1)S(1)} async-done(((f16[64,16,512]{2,1,0:T(8,128)(2,1)}), f16[64,16,512]{2,1,0:T(8,128)(2,1)S(1)}, u32[]{:S(2)}, u32[]{:S(2)}) %all-to-all-start.1) | async-done | bytes 1048608 | tf_op jit(solution)/shard_map/all_to_all | solution.py:235
  39.5 6.9 %all-to-all-start = ((f16[64,16,512]{2,1,0:T(8,128)(2,1)}), f16[64,16,512]{2,1,0:T(8,128)(2,1)}, u32[]{:S(2)}, u32[]{:S(2)}) async-start(f16[64,16,512]{2,1,0:T(8,128)(2,1)} %copy.60), calls=%async_computation | async-start | bytes 2097152 | tf_op jit(solution)/shard_map/all_to_all | solution.py:235
  46.8 1.2 multiply_reduce_fusion
  48.2 0.6 copy.66.refs_7_
  48.7 1.5 convert.7
  50.4 19.0 %all-to-all-done = f16[64,16,512]{2,1,0:T(8,128)(2,1)} async-done(((f16[64,16,512]{2,1,0:T(8,128)(2,1)}), f16[64,16,512]{2,1,0:T(8,128)(2,1)}, u32[]{:S(2)}, u32[]{:S(2)}) %all-to-all-start) | async-done | bytes 1048608 | tf_op jit(solution)/shard_map/all_to_all | solution.py:235
  69.4 1.5 convert.6
  70.9 0.3 copy.61
  71.2 0.6 copy-done.6
  71.9 7.2 %shard_map.174 = (f32[4,256,512]{2,1,0:T(8,128)S(1)}, f32[4,256,512]{2,1,0:T(8,128)S(1)}) custom-call(f32[4,256,512]{2,1,0:T(8,128)S(1)} %bitcast.62, f32[4,256,512]{2,1,0:T(8,128)S(1)} %bitcast.61, bf16[128,256]{1,0:T(8,128)(2,1)S(1)} %copy-done.9, bf16[128,256]{1,0:T(8,128)(2,1)S(1)} %copy-done.8, bf16[256,192]{1,0:T(8,128)(2,1)S(1)} %copy-done.7, ...), custom_call_target="tpu_custom_call" | custom-call | tf_op jit(solution)/shard_map/pallas_call | solution.py:123
  79.4 1.3 copy.70
  80.7 6.9 %all-to-all-start.3 = ((f16[64,16,512]{2,1,0:T(8,128)(2,1)}), f16[64,16,512]{2,1,0:T(8,128)(2,1)S(1)}, u32[]{:S(2)}, u32[]{:S(2)}) async-start(f16[64,16,512]{2,1,0:T(8,128)(2,1)} %bitcast.27), calls=%async_computation.3 | async-start | bytes 2097152 | tf_op jit(solution)/shard_map/all_to_all | solution.py:264
  87.6 1.8 broadcast_multiply_fusion.1
  89.5 0.9 reshape.90
  90.4 8.4 %broadcast_multiply_fusion = f32[32,16,32,16]{3,2,1,0:T(8,128)} fusion(f32[32,16,32,16]{3,2,1,0:T(8,128)} %constant.63, f32[16,16]{1,0:T(8,128)S(1)} %copy-done.19), kind=kLoop, calls=%fused_computation | loop fusion | flops 262144 | bytes 2098176 | tf_op jit(solution)/shard_map/mul | solution.py:199
  98.8 7.7 %reshape.94 = f32[512,512]{1,0:T(8,128)S(1)} reshape(f32[32,16,32,16]{3,2,1,0:T(8,128)} %broadcast_multiply_fusion) | data formatting | bytes 2097152 | tf_op jit(solution)/shard_map/mul | solution.py:199
  106.6 0.6 fusion.6
  107.2 0.3 copy-done.13
  107.6 1.1 fusion.2
  108.8 1.4 copy-done.3
  110.5 1.3 copy.67
  111.8 6.0 %all-to-all-start.2 = ((f16[64,16,512]{2,1,0:T(8,128)(2,1)}), f16[64,16,512]{2,1,0:T(8,128)(2,1)}, u32[]{:S(2)}, u32[]{:S(2)}) async-start(f16[64,16,512]{2,1,0:T(8,128)(2,1)} %bitcast.15), calls=%async_computation.2 | async-start | bytes 2097152 | tf_op jit(solution)/shard_map/all_to_all | solution.py:264
  117.9 0.7 multiply_bitcast_fusion.back_ref
  118.8 37.5 %shard_map.175.refs_0_ = bf16[32,512,512]{2,1,0:T(8,128)(2,1)} custom-call(bf16[32,512,512]{2,1,0:T(8,128)(2,1)} %u_ref.7, f32[16,64,512]{2,1,0:T(8,128)S(1)} %multiply_bitcast_fusion.back_ref, bf16[512,192]{1,0:T(8,128)(2,1)S(1)} %copy-done.10, bf16[2,256,256]{2,1,0:T(8,128)(2,1)S(1)} %pad_maximum_fusion.1.local_ref, ...), custom_call_target="tpu_custom_call" | custom-call | flops 17179869184 | bytes 16777216 | tf_op jit(solution)/shard_map/pallas_call | solution.py:178
  156.3 1.9 multiply_bitcast_fusion.1.back_ref
  158.2 37.5 %shard_map.176 = bf16[32,512,512]{2,1,0:T(8,128)(2,1)} custom-call(bf16[32,512,512]{2,1,0:T(8,128)(2,1)} %u_ref.7, f32[16,64,512]{2,1,0:T(8,128)S(1)} %multiply_bitcast_fusion.1.back_ref, bf16[512,192]{1,0:T(8,128)(2,1)S(1)} %copy-done.10, bf16[2,256,256]{2,1,0:T(8,128)(2,1)S(1)} %pad_maximum_fusion.1.local_ref, ...), custom_call_target="tpu_custom_call", output_to_operand_aliasing={{}: (5, {})} | custom-call | flops 17179869184 | bytes 16777216 | tf_op jit(solution)/shard_map/pallas_call | solution.py:178
  (54 shorter events, 2.3 us)
Async XLA Ops:
  0.0 46.4 %copy-start = (f32[64,16]{0,1:T(8,128)S(1)}, f32[64,16]{0,1:T(8,128)}, u32[]{:S(2)}) copy-start(f32[64,16]{0,1:T(8,128)} %param.20) | copy-start | bytes 12292
  0.0 0.9 copy-start.4
  7.4 9.1 %copy-start.5 = (bf16[128,512]{1,0:T(8,128)(2,1)S(1)}, bf16[128,512]{1,0:T(8,128)(2,1)}, u32[]{:S(2)}) copy-start(bf16[128,512]{1,0:T(8,128)(2,1)} %constant.49.clone.basis_ref) | copy-start | bytes 393220
  9.1 30.3 %all-to-all-start.1 = ((f16[64,16,512]{2,1,0:T(8,128)(2,1)}), f16[64,16,512]{2,1,0:T(8,128)(2,1)S(1)}, u32[]{:S(2)}, u32[]{:S(2)}) async-start(f16[64,16,512]{2,1,0:T(8,128)(2,1)} %copy.62), calls=%async_computation.1 | async-start | bytes 2097152 | tf_op jit(solution)/shard_map/all_to_all | solution.py:235
  23.0 23.5 %copy-start.17 = (f32[16,16,16]{2,1,0:T(8,128)S(1)}, f32[16,16,16]{2,1,0:T(8,128)}, u32[]{:S(2)}) copy-start(f32[16,16,16]{2,1,0:T(8,128)} %param.22) | copy-start | bytes 49156
  23.0 23.7 %copy-start.15 = (f32[31,16,16]{2,1,0:T(8,128)S(1)}, f32[31,16,16]{2,1,0:T(8,128)}, u32[]{:S(2)}) copy-start(f32[31,16,16]{2,1,0:T(8,128)} %constant.60) | copy-start | bytes 95236
  23.0 23.7 %copy-start.16 = (f32[64,16,16]{0,2,1:T(8,128)S(1)}, f32[64,16,16]{0,2,1:T(8,128)}, u32[]{:S(2)}) copy-start(f32[64,16,16]{0,2,1:T(8,128)} %param.19) | copy-start | bytes 196612
  39.5 7.3 %copy-start.11 = (f16[64,16,512]{2,1,0:T(8,128)(2,1)}, f16[64,16,512]{2,1,0:T(8,128)(2,1)S(1)}, u32[]{:S(2)}) copy-start(f16[64,16,512]{2,1,0:T(8,128)(2,1)S(1)} %all-to-all-done.1) | copy-start | bytes 3145732
  39.5 29.9 %all-to-all-start = ((f16[64,16,512]{2,1,0:T(8,128)(2,1)}), f16[64,16,512]{2,1,0:T(8,128)(2,1)}, u32[]{:S(2)}, u32[]{:S(2)}) async-start(f16[64,16,512]{2,1,0:T(8,128)(2,1)} %copy.60), calls=%async_computation | async-start | bytes 2097152 | tf_op jit(solution)/shard_map/all_to_all | solution.py:235
  70.9 0.9 copy-start.6
  70.9 1.0 copy-start.7
  70.9 1.0 copy-start.8
  70.9 1.0 copy-start.9
  79.1 1.6 copy-start.2
  79.3 8.2 %copy-start.18 = (f32[16,16]{1,0:T(8,128)S(1)}, f32[16,16]{1,0:T(8,128)}, u32[]{:S(2)}) copy-start(f32[16,16]{1,0:T(8,128)} %param.21) | copy-start | bytes 3076
  80.7 31.1 %all-to-all-start.3 = ((f16[64,16,512]{2,1,0:T(8,128)(2,1)}), f16[64,16,512]{2,1,0:T(8,128)(2,1)S(1)}, u32[]{:S(2)}, u32[]{:S(2)}) async-start(f16[64,16,512]{2,1,0:T(8,128)(2,1)} %bitcast.27), calls=%async_computation.3 | async-start | bytes 2097152 | tf_op jit(solution)/shard_map/all_to_all | solution.py:264
  89.4 1.0 copy-start.19
  98.8 7.7 %copy-start.14 = (f32[256,16,16]{0,2,1:T(8,128)S(1)}, f32[256,16,16]{0,2,1:T(8,128)}, u32[]{:S(2)}) copy-start(f32[256,16,16]{0,2,1:T(8,128)} %constant.62) | copy-start | bytes 786436
  98.8 7.7 %copy-start.12 = (f32[256,512]{1,0:T(8,128)S(1)}, f32[256,512]{1,0:T(8,128)}, u32[]{:S(2)}) copy-start(f32[256,512]{1,0:T(8,128)} %constant.57.clone) | copy-start | bytes 1572868
  106.5 1.0 copy-start.13
  108.7 1.6 copy-start.3
  111.8 44.5 %all-to-all-start.2 = ((f16[64,16,512]{2,1,0:T(8,128)(2,1)}), f16[64,16,512]{2,1,0:T(8,128)(2,1)}, u32[]{:S(2)}, u32[]{:S(2)}) async-start(f16[64,16,512]{2,1,0:T(8,128)(2,1)} %bitcast.15), calls=%async_computation.2 | async-start | bytes 2097152 | tf_op jit(solution)/shard_map/all_to_all | solution.py:264
  117.9 1.0 copy-start.10
  158.2 37.5 %copy-start.1 = (f32[64,16]{0,1:T(8,128)S(1)}, f32[64,16]{0,1:T(8,128)}, u32[]{:S(2)}) copy-start(f32[64,16]{0,1:T(8,128)} %param.20) | copy-start | bytes 12292
where the time goes:
time: 197 us; the launch traced here: 196 us
  Pallas kernels  94.6 us (48%)
  waiting for transfers between devices  33.7 us (17%)
  starting transfers between devices  27.2 us (14%)
  local copies, waits for them, and re-layouts  19.8 us (10%)
  other arithmetic  18.3 us (9%)
    pallas_call x2, Pallas kernels, tail(): pl.pallas_call(functools.partial(tail_kernel, math.gcd(width, 256)), grid...  75 us
    all_to_all x2, waiting for transfers between devices, shards(): lax.all_to_all(sent, 'lat', split_axis=0, concat_axis=0, tiled=True)  33.7 us
    all_to_all x2, starting transfers between devices, shards(): lax.all_to_all(sent, 'lat', split_axis=0, concat_axis=0, tiled=True)  14.3 us
    all_to_all x2, starting transfers between devices, shards(): lax.all_to_all(part, 'lat', split_axis=0, concat_axis=0, tiled=True)  12.9 us
    pallas_call x2, Pallas kernels, forward(): pl.pallas_call(forward_kernel, grid=(rows // step,), in_specs=[pl.BlockSp...  12.4 us
    mul x2, other arithmetic, block_diagonal(): return jnp.tile(small, (copies, copies)) * mask  10.3 us
    mul x2, local copies, waits for them, and re-layouts, block_diagonal(): return jnp.tile(small, (copies, copies)) * mask  8.61 us
    pallas_call x1, Pallas kernels, middle(): pl.pallas_call(functools.partial(middle_kernel, chunks, chans), grid=(cou...  7.19 us
  transfers between devices with their start and end apart: 4, of which 2 were waited for; matrix products, arithmetic and copies ran while one was open for 15% of the time, Pallas kernels for 22%

commit v1 on v0

--- a/solution.py
+++ b/solution.py
@@ -199,7 +199,7 @@
     return jnp.tile(small, (copies, copies)) * mask
 
 
-def shards(field, lat_modes, lat_gains, lat_local, depth_modes, depth_local):
+def shards_rows(field, lat_modes, lat_gains, lat_local, depth_modes, depth_local):
     highest = lax.Precision.HIGHEST
     devices = lax.axis_size("lat")
     rows_dev, width_y, cells = field.shape
@@ -269,6 +269,303 @@
         out = tail(field, part, back_y, local_pair, depth_pair, out, chunk * rows)
     return out
 
+LINK_OUT = 64.0
+LINK_BACK = 1.0 / 32.0
+C0 = 2.0 * K0
+C1 = 8.0 * K1
+
+
+def act(h):
+    return h + h * jnp.tanh(h * (C0 + C1 * (h * h)))
+
+
+def window_factors(basis, windows, fine):
+    modes = basis.shape[0]
+    blocks = basis.reshape(modes, windows, -1).transpose(1, 0, 2)
+    left, sizes, right = np.linalg.svd(blocks, full_matrices=False)
+    left = left * sizes[:, None, :]
+    top = np.abs(basis).max()
+    rank = fine
+    while rank < sizes.shape[1]:
+        product = left[:, :, :rank] @ right[:, :rank]
+        if np.abs(product - blocks).max() <= 2.0 ** -25 * top:
+            break
+        rank += fine
+    return left[:, :, :rank], right[:, :rank]
+
+
+def analysis_kernel(me_ref, basis_ref, press_ref, u_ref, out_ref, high_ref, low_ref):
+    step, modes, cells = u_ref.shape[0], basis_ref.shape[0] // 2, u_ref.shape[2]
+    at = pl.program_id(0)
+    for row in range(step):
+        both = dot(basis_ref[...], u_ref[row])
+        high, low = halves(both[:modes] + both[modes:])
+        high_ref[at * step + row] = high
+        low_ref[at * step + row] = low
+
+    @pl.when(at == pl.num_programs(0) - 1)
+    def _():
+        count = press_ref.shape[1]
+        rows = high_ref.shape[0]
+        for group in range(modes // 16):
+            take = slice(16 * group, 16 * group + 16)
+            high = high_ref[:, take, :].reshape(rows * 16, cells)
+            low = low_ref[:, take, :].reshape(rows * 16, cells)
+            stacked = jnp.concatenate([high, low, high], axis=0)
+            out_ref[count * group : count * (group + 1), :] = dot(press_ref[0], stacked)
+
+
+def analysis(field, basis, press, me):
+    rows, width, cells = field.shape
+    modes = basis.shape[0] // 2
+    step = math.gcd(rows, 4)
+    out_rows = modes // 16 * press.shape[1]
+    return pl.pallas_call(
+        analysis_kernel,
+        grid_spec=pltpu.PrefetchScalarGridSpec(
+            num_scalar_prefetch=1,
+            grid=(rows // step,),
+            in_specs=[
+                pl.BlockSpec(basis.shape, lambda i, me: (0, 0)),
+                pl.BlockSpec((1,) + press.shape[1:], lambda i, me: (me[0], 0, 0)),
+                pl.BlockSpec((step, width, cells), lambda i, me: (i, 0, 0)),
+            ],
+            out_specs=pl.BlockSpec((out_rows, cells), lambda i, me: (0, 0)),
+            scratch_shapes=[pltpu.VMEM((rows, modes, cells), jnp.bfloat16)] * 2,
+        ),
+        out_shape=jax.ShapeDtypeStruct((out_rows, cells), jnp.float32),
+        compiler_params=pltpu.CompilerParams(vmem_limit_bytes=48 * MIB),
+    )(me, basis, press, field)
+
+
+def swap(blocks, devices):
+    groups = [list(range(core, devices, 2)) for core in range(2)]
+    return lax.all_to_all(blocks, "lat", split_axis=0, concat_axis=0, axis_index_groups=groups, tiled=True)
+
+
+def turn(x, unit):
+    place = lax.broadcasted_iota(jnp.int32, (x.shape[0], 128), 1)
+    place = (128 - unit - place // unit * unit) + place % unit
+    tiles = [jnp.take_along_axis(x[:, at : at + 128], place, axis=1) for at in range(0, x.shape[1], 128)]
+    return jnp.concatenate(tiles[::-1], axis=1)
+
+
+def blend_kernel(chans, c_ref, front_ref, back_ref, gain_ref, diag_ref, out_ref):
+    modes = diag_ref.shape[1]
+    held = gain_ref.shape[0]
+    high, low = halves(c_ref[...])
+    coef = dot(front_ref[...], jnp.concatenate([high, low, high], axis=0))
+    highs, lows = [], []
+    for q in range(held):
+        part = coef[q * modes : (q + 1) * modes] * gain_ref[q]
+        tiles = []
+        for lane in range(0, part.shape[1], 128):
+            tile = part[:, lane : lane + 128]
+            total = tile * diag_ref[chans - 1]
+            for at in range(2 * chans - 1):
+                shift = at - (chans - 1)
+                if shift != 0:
+                    total += pltpu.roll(tile, (-shift) % 128, 1) * diag_ref[at]
+            tiles.append(total)
+        mixed = jnp.concatenate(tiles, axis=1)
+        half = mixed.shape[1] // 2
+        mixed = jnp.concatenate([mixed[:, :half], turn(mixed[:, half:], chans)], axis=1)
+        high, low = halves(mixed)
+        highs.append(high)
+        lows.append(low)
+    out_ref[...] = dot(back_ref[...], jnp.concatenate(highs + lows + highs, axis=0))
+
+
+def blend(coefs, front, back, gains, diags, chans):
+    whole = lambda a: pl.BlockSpec(a.shape, lambda: (0,) * a.ndim)
+    args = (coefs, front, back, gains, diags)
+    return pl.pallas_call(
+        functools.partial(blend_kernel, chans),
+        in_specs=[whole(a) for a in args],
+        out_specs=whole(coefs),
+        out_shape=jax.ShapeDtypeStruct(coefs.shape, jnp.float32),
+        compiler_params=pltpu.CompilerParams(vmem_limit_bytes=40 * MIB),
+    )(*args)
+
+
+def finish_kernel(chans, me_ref, u_ref, c_ref, grow_ref, basis_ref, local_ref, depth_ref, out_ref, high_ref, low_ref, *rhs):
+    rows, width, cells = u_ref.shape
+    half = cells // 2
+    modes = high_ref.shape[1]
+    at = pl.program_id(0)
+
+    @pl.when(at == 0)
+    def _():
+        total = high_ref.shape[0]
+        count = grow_ref.shape[2] // 3
+        for group in range(modes // 16):
+            high, low = halves(c_ref[count * group : count * (group + 1), :])
+            back = dot(grow_ref[0], jnp.concatenate([high, low, high], axis=0))
+            high, low = halves(back)
+            take = slice(16 * group, 16 * group + 16)
+            high_ref[:, take, :] = high.reshape(total, 16, cells)
+            low_ref[:, take, :] = low.reshape(total, 16, cells)
+        for r in rhs:
+            r[:, 4 * modes :, :] = local_ref[...]
+
+    def first_layer(row):
+        high, low = high_ref[at * rows + row], low_ref[at * rows + row]
+        parts = []
+        for side in range(2):
+            lanes = slice(side * half, (side + 1) * half)
+            for k, x in enumerate((high, low, high, low)):
+                rhs[row][side, modes * k : modes * (k + 1), :] = x[:, lanes]
+            u = u_ref[row, :, lanes]
+            h = dot(jnp.concatenate([basis_ref[...], u, u], axis=1), rhs[row][side])
+            wide = u.astype(jnp.float32)
+            parts.append((turn(wide, chans) if side else wide) + act(h))
+        return parts
+
+    def second_layer(row, first):
+        mixes = []
+        for side, x in enumerate((first[0] + first[1], first[0] - first[1])):
+            high, low = halves(x)
+            mixes.append(dot(jnp.concatenate([high, low, high], axis=1), depth_ref[side]))
+        upper = first[1] + act(mixes[0] - mixes[1])
+        out_ref[row, :, :half] = (first[0] + act(mixes[0] + mixes[1])).astype(out_ref.dtype)
+        out_ref[row, :, half:] = turn(upper, chans).astype(out_ref.dtype)
+
+    firsts = [first_layer(0)]
+    for row in range(rows):
+        if row + 1 < rows:
+            firsts.append(first_layer(row + 1))
+        second_layer(row, firsts[row])
+
+
+def finish(field, coefs, grow, basis, local, depth, me, chans):
+    rows, width, cells = field.shape
+    modes = basis.shape[1] // 4
+    step = math.gcd(rows, 2)
+    whole = lambda a: pl.BlockSpec(a.shape, lambda i, me: (0,) * a.ndim)
+    return pl.pallas_call(
+        functools.partial(finish_kernel, chans),
+        grid_spec=pltpu.PrefetchScalarGridSpec(
+            num_scalar_prefetch=1,
+            grid=(rows // step,),
+            in_specs=[
+                pl.BlockSpec((step, width, cells), lambda i, me: (i, 0, 0)),
+                whole(coefs),
+                pl.BlockSpec((1,) + grow.shape[1:], lambda i, me: (me[0], 0, 0)),
+                whole(basis),
+                whole(local),
+                whole(depth),
+            ],
+            out_specs=pl.BlockSpec((step, width, cells), lambda i, me: (i, 0, 0)),
+            scratch_shapes=[pltpu.VMEM((rows, modes, cells), jnp.bfloat16)] * 2
+            + [pltpu.VMEM((2, 4 * modes + cells, cells // 2), jnp.bfloat16)] * step,
+        ),
+        out_shape=jax.ShapeDtypeStruct(field.shape, jnp.bfloat16),
+        compiler_params=pltpu.CompilerParams(vmem_limit_bytes=56 * MIB),
+        cost_estimate=pl.CostEstimate(
+            flops=2 * rows * width * cells * (3 * cells),
+            bytes_accessed=4 * rows * width * cells,
+            transcendentals=2 * rows * width * cells,
+        ),
+    )(me, field, coefs, grow, basis, local, depth)
+
+
+def stack_halves(x, order, axis):
+    pair = np_halves(np.asarray(x, dtype=np.float32))
+    return np.concatenate([pair[k] for k in order], axis=axis)
+
+
+def shards_chips(devices, field, lat_modes, lat_gains, lat_local, depth_modes, depth_local):
+    highest = lax.Precision.HIGHEST
+    rows, width_y, cells = field.shape
+    modes_x, chans, _ = lat_modes.shape
+    modes_y = lat_gains.shape[0]
+    modes_z = depth_modes.shape[0]
+    depth = cells // chans
+    chips = devices // 2
+    held = modes_y // devices
+    basis_y = cosine_basis(width_y, modes_y)
+    basis_z = cosine_basis(depth, modes_z)
+    left, right = window_factors(wide_basis(rows * devices, modes_x), chips, 8 // math.gcd(held, 8))
+    rank = left.shape[2]
+    me = lax.axis_index("lat")
+    at = me.reshape(1)
+
+    own = right.reshape(chips, rank, 2, rows).transpose(0, 2, 1, 3).reshape(devices, rank, rows)
+    eye = np.eye(16)
+    press = np.einsum("djx,qr->dqjxr", own * LINK_OUT, eye).reshape(devices, 16 * rank, rows * 16)
+    press = jnp.asarray(stack_halves(press, (0, 0, 1), 2))
+    grow = np.einsum("djx,qr->dxqrj", own * (0.5 / LINK_BACK), eye).reshape(devices, rows * 16, 16 * rank)
+    grow = jnp.asarray(stack_halves(grow, (0, 0, 1), 2))
+    sides = np.einsum("ipj,qr->qpirj", left, np.eye(held)).reshape(held * modes_x, chips * held * rank)
+    front = jnp.asarray(stack_halves(sides, (0, 0, 1), 1))
+    back = jnp.asarray(stack_halves(sides.T, (0, 0, 1), 1))
+    front_y = jnp.asarray(stack_halves(basis_y, (0, 1), 0))
+    back_y = jnp.asarray(stack_halves(basis_y.T, (0, 0, 1, 1), 1))
+
+    partial = analysis(field, front_y, press, at).reshape(2, modes_y // 2 * rank, cells)
+    core = lax.rem(me, 2)
+    keep = lax.dynamic_index_in_dim(partial, core, 0, keepdims=False)
+    give = lax.dynamic_index_in_dim(partial, 1 - core, 0, keepdims=False)
+    got = lax.ppermute(give, "lat", [(d, d ^ 1) for d in range(devices)])
+    sent = (keep + got).astype(LINK).reshape(chips, held * rank, cells)
+
+    shift = np.arange(2 * chans - 1)[:, None, None] - (chans - 1)
+    places = np.arange(chans)
+    pick = (places[None, :, None] == places[None, None, :] + shift).astype(np.float32)
+    diags = jnp.sum(lat_modes[None] * pick[:, None], axis=2)
+    diags = jnp.tile(diags, (1, 1, 128 // chans))
+    first_q = core * (modes_y // 2) + me // 2 * held
+    gains = lax.dynamic_slice_in_dim(lat_gains, first_q, held, 0) * (LINK_BACK / LINK_OUT)
+    gains = jnp.tile(gains, (1, depth))[:, None, :]
+
+    folds, mixers = [], []
+    half = depth // 2
+    ids = np.arange(modes_z // 2 * chans) // chans
+    mask = (ids[:, None] == ids[None, :]).astype(np.float32)
+    for side in range(2):
+        folds.append(np.kron(basis_z[side::2, :half].T, np.eye(chans, dtype=np.float32)))
+        mixers.append(jnp.tile(depth_modes[side::2].reshape(modes_z // 2 * chans, chans), (1, modes_z // 2)) * mask)
+    folds = np.stack(folds)
+    inner = jnp.einsum("skm,snm->skn", jnp.stack(mixers), folds, precision=highest)
+    whole = jnp.einsum("snk,skm->snm", 0.5 * folds, inner, precision=highest)
+    whole = whole + 0.25 * block_diagonal(depth_local, cells // 2)[None]
+    high, low = outer_halves(whole)
+    depth_ops = jnp.concatenate([high, high, low], axis=1)
+
+    ids = np.arange(cells // 2) // chans
+    tiled = jnp.tile(0.5 * lat_local, (half, half))
+    straight = tiled * (ids[:, None] == ids[None, :]).astype(np.float32)
+    turned = tiled * (ids[:, None] == half - 1 - ids[None, :]).astype(np.float32)
+    high, low = outer_halves(jnp.stack([straight, turned]))
+    local_ops = jnp.concatenate([high, low], axis=1)
+
+    gathered = swap(sent, devices).astype(jnp.float32).reshape(chips * held * rank, cells)
+    mixed = blend(gathered, front, back, gains, diags, chans)
+    mine = swap(mixed.astype(LINK).reshape(chips, held * rank, cells), devices)
+    theirs = lax.ppermute(mine, "lat", [(d, d ^ 1) for d in range(devices)])
+    first = core == 0
+    pair = jnp.stack([jnp.where(first, mine, theirs), jnp.where(first, theirs, mine)])
+    coefs = pair.astype(jnp.float32).reshape(modes_y * rank, cells)
+    return finish(field, coefs, grow, back_y, local_ops, depth_ops, at, chans)
+
+
+def wide_basis(length, modes):
+    order = np.arange(modes, dtype=np.float64)[:, None]
+    place = np.arange(length, dtype=np.float64)[None, :]
+    scales = np.where(order == 0.0, math.sqrt(1.0 / length), math.sqrt(2.0 / length))
+    return np.cos(math.pi * order * (place + 0.5) / length) * scales
+
+
+def shards(field, lat_modes, lat_gains, lat_local, depth_modes, depth_local):
+    devices = lax.axis_size("lat")
+    rows, _, cells = field.shape
+    chans = lat_local.shape[0]
+    modes_y, modes_z = lat_gains.shape[0], depth_modes.shape[0]
+    fits = devices % 2 == 0 and modes_y % max(devices, 16) == 0 and rows % 4 == 0
+    fits = fits and modes_z % 2 == 0 and cells % 256 == 0 and cells // chans % 2 == 0
+    args = (field, lat_modes, lat_gains, lat_local, depth_modes, depth_local)
+    return shards_chips(devices, *args) if fits else shards_rows(*args)
+
 
 def solution(mesh):
     placed = (P(("group", "lat"), None, None), P(), P(), P(), P(), P())

time: 197 us -> 132 us (0.67)
  Pallas kernels: 94.6 us -> 64.9 us
  starting transfers between devices: 27.2 us -> 11.4 us
  waiting for transfers between devices: 33.7 us -> 21.8 us
  local copies, waits for them, and re-layouts: 19.8 us -> 14 us
    pallas_call x5 -> x3, Pallas kernels: 94.6 us -> 64.9 us  [the longest x1 46.8 us: finish(): pl.pallas_call(functools.partial(finish_kernel, chans), grid_spec=pltpu.P...]
    all_to_all x4 -> x2, starting transfers between devices: 27.2 us -> 10.9 us  [swap(): lax.all_to_all(blocks, 'lat', split_axis=0, concat_axis=0, axis_index_gro...]
    all_to_all x4 -> x2, waiting for transfers between devices: 33.7 us -> 18.8 us  [swap(): lax.all_to_all(blocks, 'lat', split_axis=0, concat_axis=0, axis_index_gro...]
    another operation x5 -> x11, local copies, waits for them, and re-layouts: 0.9 us -> 10.8 us  [the longest x3 4.94 us: shards_chips(): high, low = outer_halves(jnp.stack([straight, turned]))]
    mul x2 -> x1, local copies, waits for them, and re-layouts: 8.61 us -> 0.94 us  [shards_chips(): whole = whole + 0.25 * block_diagonal(depth_local, cells // 2)[None]]
    mul x6 -> x4, other arithmetic: 12.9 us -> 5.73 us  [the longest x1 5.07 us: shards_chips(): whole = whole + 0.25 * block_diagonal(depth_local, cells // 2)[None]]
    convert_element_type x2 -> x4, other arithmetic: 0.51 us -> 5.5 us  [the longest x1 2.49 us: shards_chips(): sent = (keep + got).astype(LINK).reshape(chips, held * rank, cells)]
    reshape x4 -> x0, local copies, waits for them, and re-layouts: 3.83 us -> none  [the longest x2 3.34 us: shards(): sent = sent.transpose(1, 2, 0, 3).reshape(modes_y * splits, rows, span)]
  transfers between devices with their start and end apart: 4 -> 4, of which waited for: 2 -> 3; matrix products, arithmetic and copies ran while one was open for 15% -> 17% of each run, Pallas kernels for 22% -> 0%
where the time goes in v1:
time: 132 us
  Pallas kernels  64.9 us (49%)
  waiting for transfers between devices  21.8 us (17%)
  other arithmetic  17.4 us (13%)
  local copies, waits for them, and re-layouts  14 us (11%)
  starting transfers between devices  11.4 us (9%)
  matrix products  1.92 us (1%)
    pallas_call x1, Pallas kernels, finish(): pl.pallas_call(functools.partial(finish_kernel, chans), grid_spec=pltpu.P...  46.8 us
    all_to_all x2, waiting for transfers between devices, swap(): lax.all_to_all(blocks, 'lat', split_axis=0, concat_axis=0, axis_index_gro...  18.8 us
    pallas_call x1, Pallas kernels, analysis(): pl.pallas_call(analysis_kernel, grid_spec=pltpu.PrefetchScalarGridSpec(nu...  11.8 us
    all_to_all x2, starting transfers between devices, swap(): lax.all_to_all(blocks, 'lat', split_axis=0, concat_axis=0, axis_index_gro...  10.9 us
    pallas_call x1, Pallas kernels, blend(): pl.pallas_call(functools.partial(blend_kernel, chans), in_specs=[whole(a)...  6.32 us
    mul x1, other arithmetic, shards_chips(): whole = whole + 0.25 * block_diagonal(depth_local, cells // 2)[None]  5.07 us
    another operation x3, local copies, waits for them, and re-layouts, shards_chips(): high, low = outer_halves(jnp.stack([straight, turned]))  4.94 us
    another operation x2, local copies, waits for them, and re-layouts, shards_chips(): diags = jnp.tile(diags, (1, 1, 128 // chans))  3.74 us
  transfers between devices with their start and end apart: 4, of which 3 were waited for; matrix products, arithmetic and copies ran while one was open for 17% of the time, Pallas kernels for 0%

profile of v1, /device:TPU:0, one launch (start us, length us, event | category | flops | bytes accessed | tf_op | source)
XLA Modules:
  0.0 131.7 jit_solution(2468842521479184717)
XLA Ops:
  0.0 0.9 copy-done.4
  0.9 11.8 %shard_map.181 = f32[1280,512]{1,0:T(8,128)S(1)} custom-call(s32[1]{0:T(128)} %bitcast.me_ref, bf16[128,512]{1,0:T(8,128)(2,1)S(1)} %copy-done.4, bf16[16,320,1536]{2,1,0:T(8,128)(2,1)} %constant.67.clone.press_ref, bf16[32,512,512]{2,1,0:T(8,128)(2,1)} %u_ref.3), custom_call_target="tpu_custom_call" | custom-call | tf_op jit(solution)/shard_map/pallas_call | solution.py:323
  12.7 1.2 dynamic-slice_bitcast_fusion
  13.9 0.5 collective-permute-start
  14.4 3.0 %collective-permute-done = f32[640,512]{1,0:T(8,128)} collective-permute-done((f32[640,512]{1,0:T(8,128)}, f32[640,512]{1,0:T(8,128)}, u32[]{:S(2)}, u32[]{:S(2)}) %collective-permute-start) | collective-permute-done | bytes 1310752 | tf_op jit(solution)/shard_map/ppermute | solution.py:509
  17.4 2.5 %fusion = f16[640,512]{1,0:T(8,128)(2,1)} fusion(f32[640,512]{1,0:T(8,128)} %collective-permute-done, f32[2,640,512]{2,1,0:T(8,128)S(1)} %bitcast.35, s32[]{:T(128)S(6)} %select_n.28), kind=kLoop, calls=%fused_computation.5 | loop fusion | flops 655360 | bytes 3276804 | tf_op jit(solution)/shard_map/convert_element_type | solution.py:510
  19.8 7.2 %all-to-all-start = ((f16[8,80,512]{2,1,0:T(8,128)(2,1)}), f16[8,80,512]{2,1,0:T(8,128)(2,1)}, u32[]{:S(2)}, u32[]{:S(2)}) async-start(f16[8,80,512]{2,1,0:T(8,128)(2,1)} %bitcast.4), calls=%async_computation | async-start | bytes 1310720 | tf_op jit(solution)/shard_map/all_to_all | solution.py:343
  27.2 0.1 tile.69.gain_ref
  27.5 1.2 multiply_reduce_fusion
  28.7 1.5 %tile.57 = f32[31,64,8,16]{1,3,2,0:T(8,128)} broadcast(f32[31,64,16]{1,2,0:T(8,128)S(1)} %multiply_reduce_fusion), dimensions={0,1,3} | broadcast | bytes 1142784 | tf_op jit(solution)/shard_map/tile | solution.py:516
  30.2 2.3 %copy.37.diag_ref = f32[31,64,128]{2,1,0:T(8,128)S(1)} copy(f32[31,64,128]{1,2,0:T(8,128)} %bitcast.36) | data formatting | bytes 2031616 | tf_op jit(solution)/shard_map/tile | solution.py:516
  32.5 12.2 %all-to-all-done = f16[8,80,512]{2,1,0:T(8,128)(2,1)} async-done(((f16[8,80,512]{2,1,0:T(8,128)(2,1)}), f16[8,80,512]{2,1,0:T(8,128)(2,1)}, u32[]{:S(2)}, u32[]{:S(2)}) %all-to-all-start) | async-done | bytes 655392 | tf_op jit(solution)/shard_map/all_to_all | solution.py:343
  44.8 1.2 bitcast_convert_fusion.1.c_ref
  46.0 6.3 %shard_map.182 = f32[640,512]{1,0:T(8,128)S(1)} custom-call(f32[640,512]{1,0:T(8,128)S(1)} %bitcast_convert_fusion.1.c_ref, bf16[256,1920]{1,0:T(8,128)(2,1)S(1)} %copy-done.3, bf16[640,768]{1,0:T(8,128)(2,1)S(1)} %copy-done.2, f32[4,1,512]{2,1,0:T(1,128)S(1)} %tile.69.gain_ref, f32[31,64,128]{2,1,0:T(8,128)S(1)} %copy.37.diag_ref), custom_call_target="tpu_custom_call" | custom-call | tf_op jit(solution)/shard_map/pallas_call | solution.py:382
  52.4 1.0 convert_element_type.27
  53.4 3.7 %all-to-all-start.1 = ((f16[8,80,512]{2,1,0:T(8,128)(2,1)}), f16[8,80,512]{2,1,0:T(8,128)(2,1)S(1)}, u32[]{:S(2)}, u32[]{:S(2)}) async-start(f16[8,80,512]{2,1,0:T(8,128)(2,1)} %bitcast.7), calls=%async_computation.1 | async-start | bytes 1310720 | tf_op jit(solution)/shard_map/all_to_all | solution.py:343
  57.1 5.1 %multiply_multiply_fusion = (f32[16,16,16,16]{3,2,1,0:T(8,128)S(1)}, f32[16,16,16,16]{3,2,1,0:T(8,128)}, f32[16,16,16,16]{3,2,1,0:T(8,128)}) fusion(f32[16,16,16,16]{3,2,1,0:T(8,128)} %constant.80, f32[16,16]{1,0:T(8,128)S(1)} %copy-done.10, f32[16,16]{1,0:T(8,128)S(1)} %broadcast_multiply_fusion.4, f32[16,16,16,16]{3,2,1,0:T(8,128)} %constant.81), kind=kLoop, calls=%fused_computation.1 | loop fusion | flops 262144 | bytes 1312768 | tf_op jit(solution)/shard_map/mul | solution.py:531
  62.2 2.4 %stack.30 = f32[1,256,256]{2,1,0:T(8,128)S(1)} reshape(f32[16,16,16,16]{3,2,1,0:T(8,128)} %get-tuple-element.6) | data formatting | bytes 524288 | tf_op jit(solution)/shard_map/stack | solution.py:539
  64.6 2.5 %stack.31 = f32[1,256,256]{2,1,0:T(8,128)S(1)} reshape(f32[16,16,16,16]{3,2,1,0:T(8,128)} %get-tuple-element.17) | data formatting | bytes 524288 | tf_op jit(solution)/shard_map/stack | solution.py:539
  67.2 0.7 broadcast_multiply_fusion.3
  67.9 6.6 %all-to-all-done.1 = f16[8,80,512]{2,1,0:T(8,128)(2,1)S(1)} async-done(((f16[8,80,512]{2,1,0:T(8,128)(2,1)}), f16[8,80,512]{2,1,0:T(8,128)(2,1)S(1)}, u32[]{:S(2)}, u32[]{:S(2)}) %all-to-all-start.1) | async-done | bytes 655392 | tf_op jit(solution)/shard_map/all_to_all | solution.py:343
  74.5 0.8 pad_maximum_fusion.2.local_ref
  75.3 0.9 copy.40
  76.2 0.9 copy.41
  77.2 0.9 reshape.68
  78.1 1.3 %fusion.3 = f32[2,128,256]{2,1,0:T(8,128)S(1)} fusion(f32[2,256,128]{2,1,0:T(8,128)} %constant.75.clone, f32[1,128,128]{2,1,0:T(8,128)S(1)} %copy.41, f32[1,128,128]{2,1,0:T(8,128)S(1)} %copy.40), kind=kOutput, calls=%fused_computation.21 | convolution fusion | flops 100696064 | bytes 655360 | tf_op jit(solution)/shard_map/skm,snm->skn/dot_general | solution.py:529
  79.5 0.6 reduce-precision_convert_fusion
  80.1 0.9 pad_maximum_fusion.1.depth_ref
  81.0 1.5 %select_bitcast_fusion.1 = (f16[1,8,80,512]{3,2,1,0:T(8,128)(2,1)S(1)}, f16[1,8,80,512]{3,2,1,0:T(8,128)(2,1)S(1)}) fusion(f16[8,80,512]{2,1,0:T(8,128)(2,1)S(1)} %all-to-all-done.1, f16[8,80,512]{2,1,0:T(8,128)(2,1)} %collective-permute-done.1, pred[]{:T(512)S(6)} %eq.3), kind=kLoop, calls=%fused_computation.17 | loop fusion | flops 655360 | bytes 2621441 | tf_op jit(solution)/shard_map/stack | solution.py:547
  82.5 0.3 pad_maximum_fusion
  82.9 2.0 %bitcast_convert_fusion.c_ref = f32[1280,512]{1,0:T(8,128)} fusion(f16[2,8,80,512]{3,2,1,0:T(8,128)(2,1)S(1)} %pad_maximum_fusion), kind=kLoop, calls=%fused_computation.3 | loop fusion | flops 655360 | bytes 3932160 | tf_op jit(solution)/shard_map/convert_element_type | solution.py:548
  84.8 46.8 %shard_map.183 = bf16[32,512,512]{2,1,0:T(8,128)(2,1)} custom-call(s32[1]{0:T(128)} %bitcast.me_ref, bf16[32,512,512]{2,1,0:T(8,128)(2,1)} %u_ref.3, f32[1280,512]{1,0:T(8,128)} %bitcast_convert_fusion.c_ref, bf16[16,512,960]{2,1,0:T(8,128)(2,1)} %constant.68.clone.grow_ref, bf16[512,256]{1,0:T(8,128)(2,1)} %constant.72.clone.basis_ref, ...), custom_call_target="tpu_custom_call" | custom-call | flops 25769803776 | bytes 33554432 | tf_op jit(solution)/shard_map/pallas_call | solution.py:445
  (36 shorter events, 0.5 us)
Async XLA Ops:
  0.0 27.1 %copy-start = (f32[64,16]{0,1:T(8,128)S(1)}, f32[64,16]{0,1:T(8,128)}, u32[]{:S(2)}) copy-start(f32[64,16]{0,1:T(8,128)} %param.21) | copy-start | bytes 12292
  0.0 0.9 copy-start.4
  13.9 3.5 %collective-permute-start = (f32[640,512]{1,0:T(8,128)}, f32[640,512]{1,0:T(8,128)}, u32[]{:S(2)}, u32[]{:S(2)}) collective-permute-start(f32[640,512]{1,0:T(8,128)} %dynamic-slice_bitcast_fusion), channel_id=1, source_target_pairs={{0,1},{1,0},{2,3},{3,2},{4,5},{5,4},{6,7},{7,6},{8,9},{9,8},{10,11... | collective-permute-start | bytes 3932168 | tf_op jit(solution)/shard_map/ppermute | solution.py:509
  14.3 13.0 %copy-start.8 = (f32[16,16,16]{2,1,0:T(8,128)S(1)}, f32[16,16,16]{2,1,0:T(8,128)}, u32[]{:S(2)}) copy-start(f32[16,16,16]{2,1,0:T(8,128)} %param.23) | copy-start | bytes 49156
  14.4 13.1 %copy-start.6 = (f32[31,16,16]{2,1,0:T(8,128)S(1)}, f32[31,16,16]{2,1,0:T(8,128)}, u32[]{:S(2)}) copy-start(f32[31,16,16]{2,1,0:T(8,128)} %constant.79) | copy-start | bytes 95236
  14.4 13.1 %copy-start.7 = (f32[64,16,16]{0,2,1:T(8,128)S(1)}, f32[64,16,16]{0,2,1:T(8,128)}, u32[]{:S(2)}) copy-start(f32[64,16,16]{0,2,1:T(8,128)} %param.20) | copy-start | bytes 196612
  19.8 24.9 %all-to-all-start = ((f16[8,80,512]{2,1,0:T(8,128)(2,1)}), f16[8,80,512]{2,1,0:T(8,128)(2,1)}, u32[]{:S(2)}, u32[]{:S(2)}) async-start(f16[8,80,512]{2,1,0:T(8,128)(2,1)} %bitcast.4), calls=%async_computation | async-start | bytes 1310720 | tf_op jit(solution)/shard_map/all_to_all | solution.py:343
  28.7 3.8 %copy-start.11 = (f32[16,16]{1,0:T(8,128)S(1)}, f32[16,16]{1,0:T(8,128)}, u32[]{:S(2)}) copy-start(f32[16,16]{1,0:T(8,128)} %param.22) | copy-start | bytes 3076
  30.2 15.8 %copy-start.2 = (bf16[640,768]{1,0:T(8,128)(2,1)S(1)}, bf16[640,768]{1,0:T(8,128)(2,1)}, u32[]{:S(2)}) copy-start(bf16[640,768]{1,0:T(8,128)(2,1)} %constant.70.clone.back_ref) | copy-start | bytes 2949124
  30.2 15.8 %copy-start.3 = (bf16[256,1920]{1,0:T(8,128)(2,1)S(1)}, bf16[256,1920]{1,0:T(8,128)(2,1)}, u32[]{:S(2)}) copy-start(bf16[256,1920]{1,0:T(8,128)(2,1)} %constant.69.clone.front_ref) | copy-start | bytes 2949124
  52.4 4.7 %copy-start.10 = (f32[16,16]{1,0:T(8,128)S(1)}, f32[16,16]{1,0:T(8,128)}, u32[]{:S(2)}) copy-start(f32[16,16]{1,0:T(8,128)} %param.24) | copy-start | bytes 3076
  53.4 21.1 %all-to-all-start.1 = ((f16[8,80,512]{2,1,0:T(8,128)(2,1)}), f16[8,80,512]{2,1,0:T(8,128)(2,1)S(1)}, u32[]{:S(2)}, u32[]{:S(2)}) async-start(f16[8,80,512]{2,1,0:T(8,128)(2,1)} %bitcast.7), calls=%async_computation.1 | async-start | bytes 1310720 | tf_op jit(solution)/shard_map/all_to_all | solution.py:343
  64.6 2.6 %copy-start.9 = (f32[128,8,16]{0,2,1:T(8,128)S(1)}, f32[128,8,16]{0,2,1:T(8,128)}, u32[]{:S(2)}) copy-start(f32[128,8,16]{0,2,1:T(8,128)} %constant.82) | copy-start | bytes 196612
  74.5 6.5 %collective-permute-start.1 = (f16[8,80,512]{2,1,0:T(8,128)(2,1)S(1)}, f16[8,80,512]{2,1,0:T(8,128)(2,1)}, u32[]{:S(2)}, u32[]{:S(2)}) collective-permute-start(f16[8,80,512]{2,1,0:T(8,128)(2,1)S(1)} %all-to-all-done.1), channel_id=1, source_target_pairs={{0,1},{1,0},{2,3},{3,2},{4,5},{5,4},{6,7},{7,6},{8,9},{9,8},{10,11... | collective-permute-start | bytes 1966088 | tf_op jit(solution)/shard_map/ppermute | solution.py:545
  74.5 5.0 %copy-start.5 = (f32[2,256,128]{2,1,0:T(8,128)S(1)}, f32[2,256,128]{2,1,0:T(8,128)}, u32[]{:S(2)}) copy-start(f32[2,256,128]{2,1,0:T(8,128)} %constant.76.clone) | copy-start | bytes 786436
  84.8 46.8 %copy-start.1 = (f32[64,16]{0,1:T(8,128)S(1)}, f32[64,16]{0,1:T(8,128)}, u32[]{:S(2)}) copy-start(f32[64,16]{0,1:T(8,128)} %param.21) | copy-start | bytes 12292

commit v2 on v0

--- a/solution.py
+++ b/solution.py
@@ -199,7 +199,7 @@
     return jnp.tile(small, (copies, copies)) * mask
 
 
-def shards(field, lat_modes, lat_gains, lat_local, depth_modes, depth_local):
+def shards_rows(field, lat_modes, lat_gains, lat_local, depth_modes, depth_local):
     highest = lax.Precision.HIGHEST
     devices = lax.axis_size("lat")
     rows_dev, width_y, cells = field.shape
@@ -269,6 +269,519 @@
         out = tail(field, part, back_y, local_pair, depth_pair, out, chunk * rows)
     return out
 
+LINK_OUT = 64.0
+LINK_BACK = 1.0 / 32.0
+C0 = 2.0 * K0
+C1 = 8.0 * K1
+
+
+def act(h):
+    return h + h * jnp.tanh(h * (C0 + C1 * (h * h)))
+
+
+def window_factors(basis, windows, fine):
+    modes = basis.shape[0]
+    blocks = basis.reshape(modes, windows, -1).transpose(1, 0, 2)
+    left, sizes, right = np.linalg.svd(blocks, full_matrices=False)
+    left = left * sizes[:, None, :]
+    top = np.abs(basis).max()
+    rank = fine
+    while rank < sizes.shape[1]:
+        product = left[:, :, :rank] @ right[:, :rank]
+        if np.abs(product - blocks).max() <= 2.0 ** -25 * top:
+            break
+        rank += fine
+    return left[:, :, :rank], right[:, :rank]
+
+
+def turn(x, unit):
+    place = lax.broadcasted_iota(jnp.int32, (x.shape[0], 128), 1)
+    place = (128 - unit - place // unit * unit) + place % unit
+    tiles = [jnp.take_along_axis(x[:, at : at + 128], place, axis=1) for at in range(0, x.shape[1], 128)]
+    return jnp.concatenate(tiles[::-1], axis=1)
+
+
+LEAD = 8
+CHUNK = 128
+
+
+def exact(a, b):
+    return jnp.dot(a, b, preferred_element_type=jnp.float32, precision=lax.Precision.HIGHEST)
+
+
+def block_mask(size, unit, flip):
+    row = lax.broadcasted_iota(jnp.int32, (size, size), 0) // unit
+    lane = lax.broadcasted_iota(jnp.int32, (size, size), 1) // unit
+    return (row == (size // unit - 1 - lane if flip else lane)).astype(jnp.float32)
+
+
+def exchange_kernel(chips, held, rank, chans, *refs):
+    (field, press_all, grow_all, basis, front, back, gains, modes_in, picks, folds, folds_t, sides, spread8, spread16, spread_t, depth_in,
+     depth_local, lat_local, high_out, low_out, depth_out, local_out) = refs[:22]
+    (u, press, grow, highs, lows, part, fresh, send, land, reply, home, wide_high, wide_low, diags, depth_ops, local_ops) = refs[22:38]
+    load_sem, table_sem, pair_send, pair_recv, out_send, out_recv, in_send, in_recv, hand_send, hand_recv, store_sem, ops_sem = refs[38:]
+    rows, width, cells = field.shape
+    modes = basis.shape[0] // 2
+    chunks = cells // CHUNK
+    tall, lead = held * rank, held * LEAD
+    mesh_ids = pl.DeviceIdType.MESH
+    me = lax.axis_index("lat")
+    chip, core = me // 2, lax.rem(me, 2)
+    other = chip * 2 + 1 - core
+    subs = 4
+    span = rows // subs
+
+    def load(ch, sub):
+        take = pl.ds(sub * span, span)
+        return pltpu.make_async_copy(
+            field.at[take, :, pl.ds(ch * CHUNK, CHUNK)], u.at[ch % 2, take], load_sem.at[ch, sub]
+        )
+
+    def tables():
+        return (
+            pltpu.make_async_copy(press_all.at[me], press, table_sem.at[0]),
+            pltpu.make_async_copy(grow_all.at[me], grow, table_sem.at[1]),
+        )
+
+    for sub in range(subs):
+        load(0, sub).start()
+    for copy in tables():
+        copy.start()
+    for sub in range(subs):
+        load(1, sub).start()
+
+    barrier = pltpu.get_barrier_semaphore()
+    for off in range(1, chips):
+        peer = lax.rem(chip + off, chips) * 2 + core
+        pl.semaphore_signal(barrier, inc=1, device_id={"lat": peer}, device_id_type=mesh_ids)
+    pl.semaphore_signal(barrier, inc=1, device_id={"lat": other}, device_id_type=mesh_ids)
+
+    def pair_copy(ch):
+        return pltpu.make_async_remote_copy(
+            src_ref=part.at[ch, 1 - core],
+            dst_ref=fresh.at[ch],
+            send_sem=pair_send.at[ch],
+            recv_sem=pair_recv.at[ch],
+            device_id={"lat": other},
+            device_id_type=mesh_ids,
+        )
+
+    def chip_copy(source, target, send_sems, recv_sems, ch, off):
+        to = lax.rem(chip + off, chips)
+        return pltpu.make_async_remote_copy(
+            src_ref=source.at[ch, to],
+            dst_ref=target.at[chip],
+            send_sem=send_sems.at[ch, off - 1],
+            recv_sem=recv_sems.at[ch, off - 1],
+            device_id={"lat": to * 2 + core},
+            device_id_type=mesh_ids,
+        )
+
+    def out_copy(ch, off):
+        return chip_copy(send, land.at[ch], out_send, out_recv, ch, off)
+
+    def in_copy(ch, off):
+        return chip_copy(reply, home.at[ch, core], in_send, in_recv, ch, off)
+
+    def hand_copy(ch, off):
+        slot = lax.rem(chip + chips - off, chips)
+        return pltpu.make_async_remote_copy(
+            src_ref=home.at[ch, core, slot],
+            dst_ref=home.at[ch, core, slot],
+            send_sem=hand_send.at[ch, off],
+            recv_sem=hand_recv.at[ch, off],
+            device_id={"lat": other},
+            device_id_type=mesh_ids,
+        )
+
+    def analyse(ch):
+        for sub in range(subs):
+            load(ch, sub).wait()
+
+            def body(k, carry):
+                x = sub * span + 2 * k
+                pair = jnp.concatenate([u[ch % 2, x], u[ch % 2, x + 1]], axis=1)
+                both = dot(basis[...], pair)
+                high, low = halves(both[:modes] + both[modes:])
+                for at in range(2):
+                    highs[x + at] = high[:, at * CHUNK : (at + 1) * CHUNK]
+                    lows[x + at] = low[:, at * CHUNK : (at + 1) * CHUNK]
+                return carry
+
+            lax.fori_loop(0, span // 2, body, 0, unroll=True)
+        if ch + 2 < chunks:
+            for sub in range(subs):
+                load(ch + 2, sub).start()
+        if ch == 0:
+            for copy in tables():
+                copy.wait()
+        count = press.shape[0]
+        for group in range(0, modes // 16, 2):
+            stacks = []
+            for g in (group, group + 1):
+                take = slice(16 * g, 16 * g + 16)
+                high = highs[:, take, :].reshape(rows * 16, CHUNK)
+                low = lows[:, take, :].reshape(rows * 16, CHUNK)
+                stacks.append(jnp.concatenate([high, low, high], axis=0))
+            product = dot(press[...], jnp.concatenate(stacks, axis=1))
+            half, within = divmod(group, modes // 32)
+            for at in range(2):
+                part[ch, half, count * (within + at) : count * (within + at + 1), :] = product[:, at * CHUNK : (at + 1) * CHUNK]
+
+    def spill(value, target, ch):
+        high = value.astype(jnp.bfloat16)
+        cube = value.reshape(chips, tall, CHUNK)
+        high_cube = high.reshape(chips, tall, CHUNK)
+        low = cube[:, :lead] - high_cube[:, :lead].astype(jnp.float32)
+        target[ch, :, :tall, :] = high_cube
+        target[ch, :, tall:, :] = low.astype(jnp.bfloat16)
+
+    def emit(ch):
+        pair_copy(ch).wait_recv()
+        spill(part[ch, core] + fresh[ch], send, ch)
+        for off in range(1, chips):
+            out_copy(ch, off).start()
+        land[ch, chip] = send[ch, chip]
+
+    def prepare():
+        flat = modes_in[...]
+        first = flat.astype(jnp.bfloat16)
+        rest = flat - first.astype(jnp.float32)
+        second = rest.astype(jnp.bfloat16)
+        third = (rest - second.astype(jnp.float32)).astype(jnp.bfloat16)
+        product = dot(jnp.concatenate([first, second, third], axis=0), picks[...])
+        size = flat.shape[0]
+        total = product[:size] + product[size : 2 * size] + product[2 * size :]
+        for at in range(2 * chans - 1):
+            diags[at] = total[:, at * 128 : (at + 1) * 128]
+        half = folds.shape[1]
+        local = exact(exact(spread_t[...], depth_local[...]), spread16[...]) * block_mask(half, chans, False)
+        for side in range(2):
+            mixer = exact(exact(sides[side], depth_in[...]), spread8[...]) * block_mask(folds.shape[2], chans, False)
+            whole = 0.5 * exact(exact(folds[side], mixer), folds_t[side]) + 0.25 * local
+            high, low = halves(whole)
+            for at, x in enumerate((high, high, low)):
+                depth_ops[side, at * half : (at + 1) * half, :] = x
+        spot = exact(exact(spread_t[...], lat_local[...]), spread16[...]) * 0.5
+        for side in range(2):
+            high, low = halves(spot * block_mask(half, chans, side == 1))
+            local_ops[side, :half, :] = high
+            local_ops[side, half:, :] = low
+
+    def ops_copies():
+        return (
+            pltpu.make_async_copy(depth_ops, depth_out, ops_sem.at[0]),
+            pltpu.make_async_copy(local_ops, local_out, ops_sem.at[1]),
+        )
+
+    first_q = core * (modes // 2) + chip * held
+
+    def blend(ch):
+        for off in range(1, chips):
+            out_copy(ch, off).wait_recv()
+        high = land[ch, :, :tall, :].reshape(chips * tall, CHUNK)
+        low = land[ch, :, tall:, :].reshape(chips * lead, CHUNK)
+        coef = dot(front[...], jnp.concatenate([high, high, low], axis=0))
+        scale = exact(gains[...], spread8[...])
+        size = diags.shape[1]
+        upper, lower = [], []
+        for q in range(held):
+            tile = coef[q * size : (q + 1) * size] * gains_row(scale, q)
+            total = tile * diags[chans - 1]
+            for at in range(2 * chans - 1):
+                shift = at - (chans - 1)
+                if shift != 0:
+                    total += pltpu.roll(tile, (-shift) % 128, 1) * diags[at]
+            if 2 * ch >= chunks:
+                total = turn(total, chans)
+            high, low = halves(total)
+            upper.append(high)
+            lower.append(low)
+        spill(dot(back[...], jnp.concatenate(upper + lower + upper, axis=0)), reply, ch)
+        for off in range(1, chips):
+            in_copy(ch, off).start()
+        home[ch, core, chip] = reply[ch, chip]
+        hand_copy(ch, 0).start()
+
+    def gains_row(scale, q):
+        at = lax.broadcasted_iota(jnp.int32, scale.shape, 0)
+        return jnp.sum(jnp.where(at == first_q + q, scale, 0.0), axis=0, keepdims=True)
+
+    def hand(ch):
+        for off in range(1, chips):
+            in_copy(ch, off).wait_recv()
+            hand_copy(ch, off).start()
+
+    def place(ch):
+        return ch if 2 * ch < chunks else chunks + chunks // 2 - 1 - ch
+
+    def store_copies(ch):
+        lanes = pl.ds(place(ch) * CHUNK, CHUNK)
+        return (
+            pltpu.make_async_copy(wide_high.at[ch], high_out.at[:, :, lanes], store_sem.at[ch, 0]),
+            pltpu.make_async_copy(wide_low.at[ch], low_out.at[:, :, lanes], store_sem.at[ch, 1]),
+        )
+
+    def expand(ch):
+        for off in range(chips):
+            hand_copy(ch, off).wait_recv()
+        each = 16 // held
+        for group in range(0, modes // 16, 2):
+            stacks = []
+            for g in (group, group + 1):
+                half, within = divmod(g, modes // 32)
+                take = slice(each * within, each * (within + 1))
+                high = home[ch, half, take, :tall, :].reshape(each * tall, CHUNK)
+                low = home[ch, half, take, tall:, :].reshape(each * lead, CHUNK)
+                stacks.append(jnp.concatenate([high, high, low], axis=0))
+            high, low = halves(dot(grow[...], jnp.concatenate(stacks, axis=1)))
+            for at in range(2):
+                take = slice(16 * (group + at), 16 * (group + at + 1))
+                lanes = slice(at * CHUNK, (at + 1) * CHUNK)
+                wide_high[ch, :, take, :] = high[:, lanes].reshape(rows, 16, CHUNK)
+                wide_low[ch, :, take, :] = low[:, lanes].reshape(rows, 16, CHUNK)
+        for copy in store_copies(ch):
+            copy.start()
+
+    analyse(0)
+    pl.semaphore_wait(barrier, chips)
+    pair_copy(0).start()
+    for ch in range(1, chunks):
+        analyse(ch)
+        pair_copy(ch).start()
+        emit(ch - 1)
+    emit(chunks - 1)
+    prepare()
+    for copy in ops_copies():
+        copy.start()
+    for ch in range(chunks):
+        blend(ch)
+        if ch >= 1:
+            hand(ch - 1)
+        if ch >= 2:
+            expand(ch - 2)
+    hand(chunks - 1)
+    expand(chunks - 2)
+    expand(chunks - 1)
+    for ch in range(chunks):
+        pair_copy(ch).wait_send()
+        for off in range(1, chips):
+            out_copy(ch, off).wait_send()
+            in_copy(ch, off).wait_send()
+        for off in range(chips):
+            hand_copy(ch, off).wait_send()
+        for copy in store_copies(ch):
+            copy.wait()
+    for copy in ops_copies():
+        copy.wait()
+
+
+def exchange(chips, held, rank, chans, *args):
+    field, press_all, grow_all, basis = args[:4]
+    rows, width, cells = field.shape
+    modes = basis.shape[0] // 2
+    chunks = cells // CHUNK
+    tall, lead = held * rank, held * LEAD
+    half = cells // 2
+    size = args[7].shape[0]
+    hbm = pl.BlockSpec(memory_space=pl.ANY)
+    whole = lambda a: pl.BlockSpec(a.shape, lambda: (0,) * a.ndim)
+    dma = pltpu.SemaphoreType.DMA
+    bf16, f32 = jnp.bfloat16, jnp.float32
+    blocks = (chunks, chips, tall + lead, CHUNK)
+    return pl.pallas_call(
+        functools.partial(exchange_kernel, chips, held, rank, chans),
+        in_specs=[hbm] * 3 + [whole(a) for a in args[3:]],
+        out_specs=[hbm] * 4,
+        out_shape=[
+            jax.ShapeDtypeStruct((rows, modes, cells), bf16),
+            jax.ShapeDtypeStruct((rows, modes, cells), bf16),
+            jax.ShapeDtypeStruct((2, 3 * half, half), bf16),
+            jax.ShapeDtypeStruct((2, 2 * half, half), bf16),
+        ],
+        scratch_shapes=[
+            pltpu.VMEM((2, rows, width, CHUNK), bf16),
+            pltpu.VMEM(press_all.shape[1:], bf16),
+            pltpu.VMEM(grow_all.shape[1:], bf16),
+            pltpu.VMEM((rows, modes, CHUNK), bf16),
+            pltpu.VMEM((rows, modes, CHUNK), bf16),
+            pltpu.VMEM((chunks, 2, chips * tall, CHUNK), f32),
+            pltpu.VMEM((chunks, chips * tall, CHUNK), f32),
+            pltpu.VMEM(blocks, bf16),
+            pltpu.VMEM(blocks, bf16),
+            pltpu.VMEM(blocks, bf16),
+            pltpu.VMEM((chunks, 2) + blocks[1:], bf16),
+            pltpu.VMEM((chunks, rows, modes, CHUNK), bf16),
+            pltpu.VMEM((chunks, rows, modes, CHUNK), bf16),
+            pltpu.VMEM((2 * chans - 1, size, 128), f32),
+            pltpu.VMEM((2, 3 * half, half), bf16),
+            pltpu.VMEM((2, 2 * half, half), bf16),
+            dma((chunks, 4)),
+            dma((2,)),
+            dma((chunks,)),
+            dma((chunks,)),
+            dma((chunks, chips - 1)),
+            dma((chunks, chips - 1)),
+            dma((chunks, chips - 1)),
+            dma((chunks, chips - 1)),
+            dma((chunks, chips)),
+            dma((chunks, chips)),
+            dma((chunks, 2)),
+            dma((2,)),
+        ],
+        compiler_params=pltpu.CompilerParams(collective_id=5, has_side_effects=True, vmem_limit_bytes=58 * MIB),
+    )(*args)
+
+
+def finish_kernel(chans, u_ref, high_ref, low_ref, basis_ref, local_ref, depth_ref, out_ref, *rhs):
+    rows, width, cells = u_ref.shape
+    half = cells // 2
+    modes = high_ref.shape[1]
+
+    @pl.when(pl.program_id(0) == 0)
+    def _():
+        for r in rhs:
+            r[:, 4 * modes :, :] = local_ref[...]
+
+    def first_layer(row):
+        high, low = high_ref[row], low_ref[row]
+        parts = []
+        for side in range(2):
+            lanes = slice(side * half, (side + 1) * half)
+            for k, x in enumerate((high, low, high, low)):
+                rhs[row][side, modes * k : modes * (k + 1), :] = x[:, lanes]
+            u = u_ref[row, :, lanes]
+            h = dot(jnp.concatenate([basis_ref[...], u, u], axis=1), rhs[row][side])
+            wide = u.astype(jnp.float32)
+            parts.append((turn(wide, chans) if side else wide) + act(h))
+        return parts
+
+    def second_layer(row, first):
+        mixes = []
+        for side, x in enumerate((first[0] + first[1], first[0] - first[1])):
+            high, low = halves(x)
+            mixes.append(dot(jnp.concatenate([high, low, high], axis=1), depth_ref[side]))
+        upper = first[1] + act(mixes[0] - mixes[1])
+        out_ref[row, :, :half] = (first[0] + act(mixes[0] + mixes[1])).astype(out_ref.dtype)
+        out_ref[row, :, half:] = turn(upper, chans).astype(out_ref.dtype)
+
+    firsts = [first_layer(0)]
+    for row in range(rows):
+        if row + 1 < rows:
+            firsts.append(first_layer(row + 1))
+        second_layer(row, firsts[row])
+
+
+def finish(field, high, low, basis, local, depth, chans):
+    rows, width, cells = field.shape
+    modes = high.shape[1]
+    step = math.gcd(rows, 2)
+    whole = lambda a: pl.BlockSpec(a.shape, lambda i: (0,) * a.ndim)
+    block = pl.BlockSpec((step, width, cells), lambda i: (i, 0, 0))
+    thin = pl.BlockSpec((step, modes, cells), lambda i: (i, 0, 0))
+    return pl.pallas_call(
+        functools.partial(finish_kernel, chans),
+        grid=(rows // step,),
+        in_specs=[block, thin, thin, whole(basis), whole(local), whole(depth)],
+        out_specs=block,
+        out_shape=jax.ShapeDtypeStruct(field.shape, jnp.bfloat16),
+        scratch_shapes=[pltpu.VMEM((2, 4 * modes + cells, cells // 2), jnp.bfloat16)] * step,
+        compiler_params=pltpu.CompilerParams(vmem_limit_bytes=56 * MIB),
+        cost_estimate=pl.CostEstimate(
+            flops=2 * rows * width * cells * (3 * cells),
+            bytes_accessed=4 * rows * width * cells,
+            transcendentals=2 * rows * width * cells,
+        ),
+    )(field, high, low, basis, local, depth)
+
+
+def stack_halves(x, order, axis):
+    pair = np_halves(np.asarray(x, dtype=np.float32))
+    return np.concatenate([pair[k] for k in order], axis=axis)
+
+
+def shards_chips(devices, factors, field, lat_modes, lat_gains, lat_local, depth_modes, depth_local):
+    rows, width_y, cells = field.shape
+    modes_x, chans, _ = lat_modes.shape
+    modes_y = lat_gains.shape[0]
+    modes_z = depth_modes.shape[0]
+    depth = cells // chans
+    chips = devices // 2
+    held = modes_y // devices
+    basis_y = cosine_basis(width_y, modes_y)
+    basis_z = cosine_basis(depth, modes_z)
+    left, right = factors
+    rank = left.shape[2]
+    tall, lead, each = held * rank, held * LEAD, 16 // held
+
+    order = [(q, j) for q in range(held) for j in range(LEAD)]
+    order += [(q, j) for q in range(held) for j in range(LEAD, rank)]
+    slots = np.array([q * rank + j for q, j in order])
+
+    own = right.reshape(chips, rank, 2, rows).transpose(0, 2, 1, 3).reshape(devices, rank, rows)
+    kron = np.einsum("djx,qr->dqjxr", own, np.eye(16)).reshape(devices, each, tall, rows * 16)
+    kron = kron[:, :, slots].reshape(devices, each * tall, rows * 16)
+    press = stack_halves(kron, (0, 0, 1), 2)
+    grown = np.float32(0.5 * kron.transpose(0, 2, 1))
+    high, low = np_halves(grown)
+    leads = high.reshape(devices, rows * 16, each, tall)[..., :lead].reshape(devices, rows * 16, each * lead)
+    grow = np.concatenate([high, low, leads], axis=2)
+
+    sides = np.einsum("ipj,qr->qpirj", left, np.eye(held)).reshape(held * modes_x, chips, tall)
+    sides = sides[:, :, slots]
+    flat = np.float32(sides.reshape(held * modes_x, chips * tall))
+    high, low = np_halves(flat)
+    leads = high.reshape(held * modes_x, chips, tall)[..., :lead].reshape(held * modes_x, chips * lead)
+    front = np.concatenate([high, low, leads], axis=1)
+    back = stack_halves(flat.T, (0, 0, 1), 1)
+    front_y = stack_halves(basis_y, (0, 1), 0)
+    back_y = stack_halves(basis_y.T, (0, 0, 1, 1), 1)
+
+    places = np.arange(chans)
+    shift = np.arange(2 * chans - 1) - (chans - 1)
+    pick = (places[:, None, None, None] == (places[None, None, None, :] + shift[None, None, :, None])) & (
+        places[None, :, None, None] == places[None, None, None, :]
+    )
+    picks = np.tile(pick.reshape(chans * chans, 2 * chans - 1, chans), (1, 1, 128 // chans))
+    picks = picks.reshape(chans * chans, -1).astype(jnp.bfloat16)
+
+    half = depth // 2
+    folds = np.stack([np.kron(basis_z[side::2, :half].T, np.eye(chans)) for side in range(2)]).astype(np.float32)
+    kinds = np.eye(modes_z)
+    sides_z = np.stack([np.kron(kinds[side::2], np.eye(chans)) for side in range(2)]).astype(np.float32)
+    spread8 = np.tile(np.eye(chans, dtype=np.float32), (1, modes_z // 2))
+    spread16 = np.tile(np.eye(chans, dtype=np.float32), (1, half))
+
+    consts = [jnp.asarray(a) for a in (press, grow, front_y, front, back)]
+    more = [jnp.asarray(a) for a in (picks, folds, folds.transpose(0, 2, 1).copy(), sides_z, spread8, spread16, spread16.T.copy())]
+    args = [field] + consts + [lat_gains, lat_modes.reshape(modes_x, chans * chans)] + more
+    args += [depth_modes.reshape(modes_z * chans, chans), depth_local, lat_local]
+    high, low, depth_ops, local_ops = exchange(chips, held, rank, chans, *args)
+    return finish(field, high, low, jnp.asarray(back_y), local_ops, depth_ops, chans)
+
+
+def wide_basis(length, modes):
+    order = np.arange(modes, dtype=np.float64)[:, None]
+    place = np.arange(length, dtype=np.float64)[None, :]
+    scales = np.where(order == 0.0, math.sqrt(1.0 / length), math.sqrt(2.0 / length))
+    return np.cos(math.pi * order * (place + 0.5) / length) * scales
+
+
+def shards(field, lat_modes, lat_gains, lat_local, depth_modes, depth_local):
+    devices = lax.axis_size("lat")
+    rows, _, cells = field.shape
+    modes_x, chans, _ = lat_modes.shape
+    modes_y, modes_z = lat_gains.shape[0], depth_modes.shape[0]
+    args = (field, lat_modes, lat_gains, lat_local, depth_modes, depth_local)
+    fits = devices % 2 == 0 and modes_y % (2 * devices) == 0 and modes_y % 64 == 0 and 16 % (modes_y // devices) == 0
+    fits = fits and rows % 8 == 0 and cells % (4 * CHUNK) == 0 and chans * modes_z == 256 and cells == 512 and chans * chans == 256
+    if fits:
+        held = modes_y // devices
+        factors = window_factors(wide_basis(rows * devices, modes_x), devices // 2, max(1, 16 // held))
+        if factors[0].shape[2] >= LEAD and held * LEAD % 16 == 0:
+            return shards_chips(devices, factors, *args)
+    return shards_rows(*args)
+
 
 def solution(mesh):
     placed = (P(("group", "lat"), None, None), P(), P(), P(), P(), P())

time: 197 us -> 104 us (0.53)
  waiting for transfers between devices: 33.7 us -> 0 us
  starting transfers between devices: 27.2 us -> 0 us
  other arithmetic: 18.3 us -> 0 us
  local copies, waits for them, and re-layouts: 19.8 us -> 3.01 us
  Pallas kernels: 94.6 us -> 101 us
    all_to_all x4 -> x0, waiting for transfers between devices: 33.7 us -> none  [the longest x2 33.7 us: shards(): lax.all_to_all(sent, 'lat', split_axis=0, concat_axis=0, tiled=True)]
    all_to_all x4 -> x0, starting transfers between devices: 27.2 us -> none  [the longest x2 14.3 us: shards(): lax.all_to_all(sent, 'lat', split_axis=0, concat_axis=0, tiled=True)]
    mul x6 -> x0, other arithmetic: 12.9 us -> none  [the longest x2 10.3 us: block_diagonal(): return jnp.tile(small, (copies, copies)) * mask]
    mul x2 -> x0, local copies, waits for them, and re-layouts: 8.61 us -> none  [block_diagonal(): return jnp.tile(small, (copies, copies)) * mask]
    pallas_call x5 -> x2, Pallas kernels: 94.6 us -> 101 us  [the longest x1 57.1 us: exchange(): pl.pallas_call(functools.partial(exchange_kernel, chips, held, rank, chan...]
    reshape x4 -> x0, other arithmetic: 3.5 us -> none  [the longest x2 2.96 us: shards(): received.append(got.reshape(held, devices * rows, span))]
    transpose x2 -> x0, local copies, waits for them, and re-layouts: 2.65 us -> none  [shards(): part.astype(LINK).reshape(held, devices, rows, span).transpose(1, 0, 2, 3)]
    unnamed x41 -> x1, local copies, waits for them, and re-layouts: 3.7 us -> 1.39 us
  transfers between devices with their start and end apart: 4 -> 0, of which waited for: 2 -> 0; matrix products, arithmetic and copies ran while one was open for 15% -> 0% of each run, Pallas kernels for 22% -> 0%
where the time goes in v2:
time: 104 us
  Pallas kernels  101 us (97%)
  local copies, waits for them, and re-layouts  3.01 us (3%)
    pallas_call x1, Pallas kernels, exchange(): pl.pallas_call(functools.partial(exchange_kernel, chips, held, rank, chan...  57.1 us
    pallas_call x1, Pallas kernels, finish(): pl.pallas_call(functools.partial(finish_kernel, chans), grid=(rows // ste...  43.6 us

profile of v2, /device:TPU:0, one launch (start us, length us, event | category | flops | bytes accessed | tf_op | source)
XLA Modules:
  0.0 103.7 jit_solution(8910943645844045089)
XLA Ops:
  0.0 1.4 %copy.22.refs_6_ = f32[64,16]{1,0:T(8,128)} copy(f32[64,16]{0,1:T(8,128)} %param.21) | data formatting | bytes 8192 | tf_op args[2]
  1.4 1.6 %copy.23.refs_7_ = f32[64,256]{1,0:T(8,128)} copy(f32[64,256]{0,1:T(8,128)} %bitcast.3) | data formatting | bytes 131072 | tf_op jit(solution)/shard_map/reshape | solution.py:757
  3.0 57.1 %shard_map.181 = (bf16[32,64,512]{2,1,0:T(8,128)(2,1)}, bf16[32,64,512]{2,1,0:T(8,128)(2,1)}, bf16[2,768,256]{2,1,0:T(8,128)(2,1)}, bf16[2,512,256]{2,1,0:T(8,128)(2,1)}) custom-call(bf16[32,512,512]{2,1,0:T(8,128)(2,1)} %u_ref.1, bf16[16,320,1536]{2,1,0:T(8,128)(2,1)} %constant.26.clone.refs_1_, bf16[16,512,768]{2,1,0:T(8,128)(2,1)} %constant.27.clone.refs_2_, ...), custom_call_target="tpu_custom_call" | custom-call | tf_op jit(solution)/shard_map/pallas_call | solution.py:592
  60.1 43.6 %shard_map.182 = bf16[32,512,512]{2,1,0:T(8,128)(2,1)} custom-call(bf16[32,512,512]{2,1,0:T(8,128)(2,1)} %u_ref.1, bf16[32,64,512]{2,1,0:T(8,128)(2,1)} %get-tuple-element.9.high_ref, bf16[32,64,512]{2,1,0:T(8,128)(2,1)} %get-tuple-element.10.low_ref, bf16[512,256]{1,0:T(8,128)(2,1)} %constant.38.clone.basis_ref, ...), custom_call_target="tpu_custom_call" | custom-call | flops 25769803776 | bytes 33554432 | tf_op jit(solution)/shard_map/pallas_call | solution.py:682

commit v3 on v2

--- a/solution.py
+++ b/solution.py
@@ -288,7 +288,7 @@
     rank = fine
     while rank < sizes.shape[1]:
         product = left[:, :, :rank] @ right[:, :rank]
-        if np.abs(product - blocks).max() <= 2.0 ** -25 * top:
+        if np.abs(product - blocks).max() <= 2.0 ** -23 * top:
             break
         rank += fine
     return left[:, :, :rank], right[:, :rank]
@@ -301,12 +301,16 @@
     return jnp.concatenate(tiles[::-1], axis=1)
 
 
-LEAD = 8
+LEAD = 9
 CHUNK = 128
 
 
 def exact(a, b):
     return jnp.dot(a, b, preferred_element_type=jnp.float32, precision=lax.Precision.HIGHEST)
+
+
+def turned_dot(a, b, precision=None):
+    return lax.dot_general(a, b, (((0,), (0,)), ((), ())), precision=precision, preferred_element_type=jnp.float32)
 
 
 def block_mask(size, unit, flip):
@@ -315,15 +319,16 @@
     return (row == (size // unit - 1 - lane if flip else lane)).astype(jnp.float32)
 
 
-def exchange_kernel(chips, held, rank, chans, *refs):
-    (field, press_all, grow_all, basis, front, back, gains, modes_in, picks, folds, folds_t, sides, spread8, spread16, spread_t, depth_in,
-     depth_local, lat_local, high_out, low_out, depth_out, local_out) = refs[:22]
-    (u, press, grow, highs, lows, part, fresh, send, land, reply, home, wide_high, wide_low, diags, depth_ops, local_ops) = refs[22:38]
-    load_sem, table_sem, pair_send, pair_recv, out_send, out_recv, in_send, in_recv, hand_send, hand_recv, store_sem, ops_sem = refs[38:]
+def exchange_kernel(chips, held, tall, chans, *refs):
+    field, press_all, grow_all, front_in, back_in, picks_in, folds_in, folds_t_in, sides_in = refs[:9]
+    (basis, gains, modes_in, spread8, spread16, spread_t, depth_in, depth_local, lat_local, high_out, low_out, depth_out, local_out) = refs[9:22]
+    (u, highs, lows, part, fresh, send, land, reply, home, wide_high, wide_low, diags, depth_ops, local_ops) = refs[22:36]
+    press, grow, front, back, picks, folds, folds_t, sides = refs[36:44]
+    load_sem, table_sem, pair_send, pair_recv, out_send, out_recv, in_send, in_recv, hand_send, hand_recv, store_sem, ops_sem = refs[44:]
     rows, width, cells = field.shape
     modes = basis.shape[0] // 2
     chunks = cells // CHUNK
-    tall, lead = held * rank, held * LEAD
+    block = send.shape[2]
     mesh_ids = pl.DeviceIdType.MESH
     me = lax.axis_index("lat")
     chip, core = me // 2, lax.rem(me, 2)
@@ -338,17 +343,18 @@
         )
 
     def tables():
-        return (
-            pltpu.make_async_copy(press_all.at[me], press, table_sem.at[0]),
-            pltpu.make_async_copy(grow_all.at[me], grow, table_sem.at[1]),
-        )
+        sources = (press_all.at[me], grow_all.at[me], front_in, back_in, picks_in, folds_in, folds_t_in, sides_in)
+        targets = (press, grow, front, back, picks, folds, folds_t, sides)
+        pairs = enumerate(zip(sources, targets))
+        return [pltpu.make_async_copy(source, target, table_sem.at[k]) for k, (source, target) in pairs]
 
     for sub in range(subs):
         load(0, sub).start()
-    for copy in tables():
-        copy.start()
+    tables()[0].start()
     for sub in range(subs):
         load(1, sub).start()
+    for copy in tables()[1:]:
+        copy.start()
 
     barrier = pltpu.get_barrier_semaphore()
     for off in range(1, chips):
@@ -413,8 +419,7 @@
             for sub in range(subs):
                 load(ch + 2, sub).start()
         if ch == 0:
-            for copy in tables():
-                copy.wait()
+            tables()[0].wait()
         count = press.shape[0]
         for group in range(0, modes // 16, 2):
             stacks = []
@@ -429,12 +434,9 @@
                 part[ch, half, count * (within + at) : count * (within + at + 1), :] = product[:, at * CHUNK : (at + 1) * CHUNK]
 
     def spill(value, target, ch):
-        high = value.astype(jnp.bfloat16)
-        cube = value.reshape(chips, tall, CHUNK)
-        high_cube = high.reshape(chips, tall, CHUNK)
-        low = cube[:, :lead] - high_cube[:, :lead].astype(jnp.float32)
-        target[ch, :, :tall, :] = high_cube
-        target[ch, :, tall:, :] = low.astype(jnp.bfloat16)
+        high, low = halves(value)
+        place = lax.broadcasted_iota(jnp.int32, value.shape, 0) % block
+        target[ch] = jnp.where(place < tall, high, low).reshape(chips, block, CHUNK)
 
     def emit(ch):
         pair_copy(ch).wait_recv()
@@ -444,14 +446,12 @@
         land[ch, chip] = send[ch, chip]
 
     def prepare():
-        flat = modes_in[...]
-        first = flat.astype(jnp.bfloat16)
-        rest = flat - first.astype(jnp.float32)
-        second = rest.astype(jnp.bfloat16)
-        third = (rest - second.astype(jnp.float32)).astype(jnp.bfloat16)
-        product = dot(jnp.concatenate([first, second, third], axis=0), picks[...])
-        size = flat.shape[0]
-        total = product[:size] + product[size : 2 * size] + product[2 * size :]
+        rest, total = modes_in[...], None
+        for _ in range(3):
+            term = rest.astype(jnp.bfloat16)
+            rest = rest - term.astype(jnp.float32)
+            product = turned_dot(term, picks[...])
+            total = product if total is None else total + product
         for at in range(2 * chans - 1):
             diags[at] = total[:, at * 128 : (at + 1) * 128]
         half = folds.shape[1]
@@ -479,10 +479,9 @@
     def blend(ch):
         for off in range(1, chips):
             out_copy(ch, off).wait_recv()
-        high = land[ch, :, :tall, :].reshape(chips * tall, CHUNK)
-        low = land[ch, :, tall:, :].reshape(chips * lead, CHUNK)
-        coef = dot(front[...], jnp.concatenate([high, high, low], axis=0))
-        scale = exact(gains[...], spread8[...])
+        values = land[ch].reshape(chips * block, CHUNK)
+        coef = dot(front[...], jnp.concatenate([values, values], axis=0))
+        scale = turned_dot(gains[...], spread8[...], lax.Precision.HIGHEST)
         size = diags.shape[1]
         upper, lower = [], []
         for q in range(held):
@@ -531,9 +530,8 @@
             for g in (group, group + 1):
                 half, within = divmod(g, modes // 32)
                 take = slice(each * within, each * (within + 1))
-                high = home[ch, half, take, :tall, :].reshape(each * tall, CHUNK)
-                low = home[ch, half, take, tall:, :].reshape(each * lead, CHUNK)
-                stacks.append(jnp.concatenate([high, high, low], axis=0))
+                values = home[ch, half, take].reshape(each * block, CHUNK)
+                stacks.append(jnp.concatenate([values, values], axis=0))
             high, low = halves(dot(grow[...], jnp.concatenate(stacks, axis=1)))
             for at in range(2):
                 take = slice(16 * (group + at), 16 * (group + at + 1))
@@ -546,22 +544,24 @@
     analyse(0)
     pl.semaphore_wait(barrier, chips)
     pair_copy(0).start()
+    emit(0)
     for ch in range(1, chunks):
         analyse(ch)
         pair_copy(ch).start()
-        emit(ch - 1)
+        if ch > 1:
+            emit(ch - 1)
     emit(chunks - 1)
+    for copy in tables()[1:]:
+        copy.wait()
     prepare()
     for copy in ops_copies():
         copy.start()
     for ch in range(chunks):
         blend(ch)
+    for ch in range(chunks):
+        hand(ch)
         if ch >= 1:
-            hand(ch - 1)
-        if ch >= 2:
-            expand(ch - 2)
-    hand(chunks - 1)
-    expand(chunks - 2)
+            expand(ch - 1)
     expand(chunks - 1)
     for ch in range(chunks):
         pair_copy(ch).wait_send()
@@ -576,22 +576,22 @@
         copy.wait()
 
 
-def exchange(chips, held, rank, chans, *args):
-    field, press_all, grow_all, basis = args[:4]
+def exchange(chips, held, tall, block, chans, *args):
+    field, press_all, grow_all = args[:3]
+    basis, gains = args[9:11]
     rows, width, cells = field.shape
     modes = basis.shape[0] // 2
     chunks = cells // CHUNK
-    tall, lead = held * rank, held * LEAD
     half = cells // 2
-    size = args[7].shape[0]
+    size = args[11].shape[1]
     hbm = pl.BlockSpec(memory_space=pl.ANY)
     whole = lambda a: pl.BlockSpec(a.shape, lambda: (0,) * a.ndim)
     dma = pltpu.SemaphoreType.DMA
     bf16, f32 = jnp.bfloat16, jnp.float32
-    blocks = (chunks, chips, tall + lead, CHUNK)
+    blocks = (chunks, chips, block, CHUNK)
     return pl.pallas_call(
-        functools.partial(exchange_kernel, chips, held, rank, chans),
-        in_specs=[hbm] * 3 + [whole(a) for a in args[3:]],
+        functools.partial(exchange_kernel, chips, held, tall, chans),
+        in_specs=[hbm] * 9 + [whole(a) for a in args[9:]],
         out_specs=[hbm] * 4,
         out_shape=[
             jax.ShapeDtypeStruct((rows, modes, cells), bf16),
@@ -601,12 +601,10 @@
         ],
         scratch_shapes=[
             pltpu.VMEM((2, rows, width, CHUNK), bf16),
-            pltpu.VMEM(press_all.shape[1:], bf16),
-            pltpu.VMEM(grow_all.shape[1:], bf16),
             pltpu.VMEM((rows, modes, CHUNK), bf16),
             pltpu.VMEM((rows, modes, CHUNK), bf16),
-            pltpu.VMEM((chunks, 2, chips * tall, CHUNK), f32),
-            pltpu.VMEM((chunks, chips * tall, CHUNK), f32),
+            pltpu.VMEM((chunks, 2, chips * block, CHUNK), f32),
+            pltpu.VMEM((chunks, chips * block, CHUNK), f32),
             pltpu.VMEM(blocks, bf16),
             pltpu.VMEM(blocks, bf16),
             pltpu.VMEM(blocks, bf16),
@@ -616,8 +614,11 @@
             pltpu.VMEM((2 * chans - 1, size, 128), f32),
             pltpu.VMEM((2, 3 * half, half), bf16),
             pltpu.VMEM((2, 2 * half, half), bf16),
+            pltpu.VMEM(press_all.shape[1:], bf16),
+            pltpu.VMEM(grow_all.shape[1:], bf16),
+            *[pltpu.VMEM(a.shape, a.dtype) for a in args[3:9]],
             dma((chunks, 4)),
-            dma((2,)),
+            dma((8,)),
             dma((chunks,)),
             dma((chunks,)),
             dma((chunks, chips - 1)),
@@ -712,27 +713,26 @@
     basis_z = cosine_basis(depth, modes_z)
     left, right = factors
     rank = left.shape[2]
-    tall, lead, each = held * rank, held * LEAD, 16 // held
-
-    order = [(q, j) for q in range(held) for j in range(LEAD)]
-    order += [(q, j) for q in range(held) for j in range(LEAD, rank)]
-    slots = np.array([q * rank + j for q, j in order])
+    lead = lead_rows(held, rank)
+    tall, block, each = held * rank, held * (rank + lead), 16 // held
+
+    slots = [q * rank + j for q in range(held) for j in range(rank)]
+    slots = np.array(slots + [q * rank + j for q in range(held) for j in range(lead)])
+    full = (np.arange(block) < tall).astype(np.float32)
 
     own = right.reshape(chips, rank, 2, rows).transpose(0, 2, 1, 3).reshape(devices, rank, rows)
     kron = np.einsum("djx,qr->dqjxr", own, np.eye(16)).reshape(devices, each, tall, rows * 16)
-    kron = kron[:, :, slots].reshape(devices, each * tall, rows * 16)
+    kron = kron[:, :, slots].reshape(devices, each * block, rows * 16)
     press = stack_halves(kron, (0, 0, 1), 2)
-    grown = np.float32(0.5 * kron.transpose(0, 2, 1))
-    high, low = np_halves(grown)
-    leads = high.reshape(devices, rows * 16, each, tall)[..., :lead].reshape(devices, rows * 16, each * lead)
-    grow = np.concatenate([high, low, leads], axis=2)
+    high, low = np_halves(np.float32(0.5 * kron.transpose(0, 2, 1)))
+    low = (low.astype(np.float32) * np.tile(full, each)).astype(jnp.bfloat16)
+    grow = np.concatenate([high, low], axis=2)
 
     sides = np.einsum("ipj,qr->qpirj", left, np.eye(held)).reshape(held * modes_x, chips, tall)
-    sides = sides[:, :, slots]
-    flat = np.float32(sides.reshape(held * modes_x, chips * tall))
+    flat = np.float32(sides[:, :, slots].reshape(held * modes_x, chips * block))
     high, low = np_halves(flat)
-    leads = high.reshape(held * modes_x, chips, tall)[..., :lead].reshape(held * modes_x, chips * lead)
-    front = np.concatenate([high, low, leads], axis=1)
+    low = (low.astype(np.float32) * np.tile(full, chips)).astype(jnp.bfloat16)
+    front = np.concatenate([high, low], axis=1)
     back = stack_halves(flat.T, (0, 0, 1), 1)
     front_y = stack_halves(basis_y, (0, 1), 0)
     back_y = stack_halves(basis_y.T, (0, 0, 1, 1), 1)
@@ -752,12 +752,20 @@
     spread8 = np.tile(np.eye(chans, dtype=np.float32), (1, modes_z // 2))
     spread16 = np.tile(np.eye(chans, dtype=np.float32), (1, half))
 
-    consts = [jnp.asarray(a) for a in (press, grow, front_y, front, back)]
-    more = [jnp.asarray(a) for a in (picks, folds, folds.transpose(0, 2, 1).copy(), sides_z, spread8, spread16, spread16.T.copy())]
-    args = [field] + consts + [lat_gains, lat_modes.reshape(modes_x, chans * chans)] + more
+    tables = [press, grow, front, back, picks, folds, folds.transpose(0, 2, 1).copy(), sides_z]
+    args = [field] + [jnp.asarray(a) for a in tables] + [jnp.asarray(front_y), lat_gains.T]
+    args += [lat_modes.transpose(1, 2, 0).reshape(chans * chans, modes_x)]
+    args += [jnp.asarray(a) for a in (spread8, spread16, spread16.T.copy())]
     args += [depth_modes.reshape(modes_z * chans, chans), depth_local, lat_local]
-    high, low, depth_ops, local_ops = exchange(chips, held, rank, chans, *args)
+    high, low, depth_ops, local_ops = exchange(chips, held, tall, block, chans, *args)
     return finish(field, high, low, jnp.asarray(back_y), local_ops, depth_ops, chans)
+
+
+def lead_rows(held, rank):
+    lead = LEAD
+    while held * (rank + lead) % 16:
+        lead += 1
+    return lead
 
 
 def wide_basis(length, modes):
@@ -777,8 +785,9 @@
     fits = fits and rows % 8 == 0 and cells % (4 * CHUNK) == 0 and chans * modes_z == 256 and cells == 512 and chans * chans == 256
     if fits:
         held = modes_y // devices
-        factors = window_factors(wide_basis(rows * devices, modes_x), devices // 2, max(1, 16 // held))
-        if factors[0].shape[2] >= LEAD and held * LEAD % 16 == 0:
+        factors = window_factors(wide_basis(rows * devices, modes_x), devices // 2, 1)
+        rank = factors[0].shape[2]
+        if rank >= lead_rows(held, rank):
             return shards_chips(devices, factors, *args)
     return shards_rows(*args)
 

time: 104 us -> 99.6 us (0.958)
  local copies, waits for them, and re-layouts: 3.01 us -> 0 us
  Pallas kernels: 101 us -> 99.4 us
    reshape x1 -> x0, local copies, waits for them, and re-layouts: 1.62 us -> none  [shards_chips(): lat_modes.reshape(modes_x, chans * chans)]
    unnamed x1 -> x0, local copies, waits for them, and re-layouts: 1.39 us -> none
    pallas_call x1, Pallas kernels: 57.1 us -> 55.8 us  [exchange(): pl.pallas_call(functools.partial(exchange_kernel, chips, held, tall, chan...]
where the time goes in v3:
time: 99.6 us; the launch traced here: 99.4 us
  Pallas kernels  99.4 us (100%)
    pallas_call x1, Pallas kernels, exchange(): pl.pallas_call(functools.partial(exchange_kernel, chips, held, tall, chan...  55.8 us
    pallas_call x1, Pallas kernels, finish(): pl.pallas_call(functools.partial(finish_kernel, chans), grid=(rows // ste...  43.6 us

profile of v3, /device:TPU:0, one launch (start us, length us, event | category | flops | bytes accessed | tf_op | source)
XLA Modules:
  0.0 99.4 jit_solution(5714522598321595472)
XLA Ops:
  0.0 55.8 %shard_map.181 = (bf16[32,64,512]{2,1,0:T(8,128)(2,1)}, bf16[32,64,512]{2,1,0:T(8,128)(2,1)}, bf16[2,768,256]{2,1,0:T(8,128)(2,1)}, bf16[2,512,256]{2,1,0:T(8,128)(2,1)}) custom-call(bf16[32,512,512]{2,1,0:T(8,128)(2,1)} %u_ref.1, bf16[16,448,1536]{2,1,0:T(8,128)(2,1)} %constant.26.clone.refs_1_, bf16[16,512,896]{2,1,0:T(8,128)(2,1)} %constant.27.clone.refs_2_, ...), custom_call_target="tpu_custom_call" | custom-call | tf_op jit(solution)/shard_map/pallas_call | solution.py:592
  55.9 43.6 %shard_map.182 = bf16[32,512,512]{2,1,0:T(8,128)(2,1)} custom-call(bf16[32,512,512]{2,1,0:T(8,128)(2,1)} %u_ref.1, bf16[32,64,512]{2,1,0:T(8,128)(2,1)} %get-tuple-element.9.high_ref, bf16[32,64,512]{2,1,0:T(8,128)(2,1)} %get-tuple-element.10.low_ref, bf16[512,256]{1,0:T(8,128)(2,1)} %constant.38.clone.basis_ref, ...), custom_call_target="tpu_custom_call" | custom-call | flops 25769803776 | bytes 33554432 | tf_op jit(solution)/shard_map/pallas_call | solution.py:683

commit v4 on v3

--- a/solution.py
+++ b/solution.py
@@ -303,6 +303,7 @@
 
 LEAD = 9
 CHUNK = 128
+ORDER = (0, 3, 1, 2)
 
 
 def exact(a, b):
@@ -311,6 +312,13 @@
 
 def turned_dot(a, b, precision=None):
     return lax.dot_general(a, b, (((0,), (0,)), ((), ())), precision=precision, preferred_element_type=jnp.float32)
+
+
+def quarter_mask(size, unit):
+    half = size // unit // 2
+    row = lax.broadcasted_iota(jnp.int32, (size, size), 0) // unit
+    lane = lax.broadcasted_iota(jnp.int32, (size, size), 1) // unit
+    return (row == jnp.where(lane < half, lane, 3 * half - 1 - lane)).astype(jnp.float32)
 
 
 def block_mask(size, unit, flip):
@@ -321,10 +329,11 @@
 
 def exchange_kernel(chips, held, tall, chans, *refs):
     field, press_all, grow_all, front_in, back_in, picks_in, folds_in, folds_t_in, sides_in = refs[:9]
-    (basis, gains, modes_in, spread8, spread16, spread_t, depth_in, depth_local, lat_local, high_out, low_out, depth_out, local_out) = refs[9:22]
-    (u, highs, lows, part, fresh, send, land, reply, home, wide_high, wide_low, diags, depth_ops, local_ops) = refs[22:36]
-    press, grow, front, back, picks, folds, folds_t, sides = refs[36:44]
-    load_sem, table_sem, pair_send, pair_recv, out_send, out_recv, in_send, in_recv, hand_send, hand_recv, store_sem, ops_sem = refs[44:]
+    basis, gains, modes_in, spread8, spread16, spread_t, depth_in, depth_local, lat_local, synth = refs[9:19]
+    high_out, low_out, depth_out, local_out, early_out = refs[19:24]
+    (u, highs, lows, part, fresh, send, land, reply, home, wide_high, wide_low, diags, depth_ops, local_ops, firsts, rhs) = refs[24:40]
+    press, grow, front, back, picks, folds, folds_t, sides = refs[40:48]
+    load_sem, table_sem, pair_send, pair_recv, out_send, out_recv, in_send, in_recv, hand_send, hand_recv, store_sem, ops_sem, again_sem, early_sem = refs[48:]
     rows, width, cells = field.shape
     modes = basis.shape[0] // 2
     chunks = cells // CHUNK
@@ -339,7 +348,7 @@
     def load(ch, sub):
         take = pl.ds(sub * span, span)
         return pltpu.make_async_copy(
-            field.at[take, :, pl.ds(ch * CHUNK, CHUNK)], u.at[ch % 2, take], load_sem.at[ch, sub]
+            field.at[take, :, pl.ds(ORDER[ch] * CHUNK, CHUNK)], u.at[ch % 2, take], load_sem.at[ch, sub]
         )
 
     def tables():
@@ -463,10 +472,12 @@
             for at, x in enumerate((high, high, low)):
                 depth_ops[side, at * half : (at + 1) * half, :] = x
         spot = exact(exact(spread_t[...], lat_local[...]), spread16[...]) * 0.5
-        for side in range(2):
-            high, low = halves(spot * block_mask(half, chans, side == 1))
-            local_ops[side, :half, :] = high
-            local_ops[side, half:, :] = low
+        high, low = halves(spot * quarter_mask(half, chans))
+        local_ops[:half, :] = high
+        local_ops[half:, :] = low
+        for slot in range(2):
+            rhs[slot, 4 * modes : 4 * modes + half, :] = high
+            rhs[slot, 4 * modes + half :, :] = low
 
     def ops_copies():
         return (
@@ -491,7 +502,7 @@
                 shift = at - (chans - 1)
                 if shift != 0:
                     total += pltpu.roll(tile, (-shift) % 128, 1) * diags[at]
-            if 2 * ch >= chunks:
+            if 2 * ORDER[ch] >= chunks:
                 total = turn(total, chans)
             high, low = halves(total)
             upper.append(high)
@@ -511,15 +522,41 @@
             in_copy(ch, off).wait_recv()
             hand_copy(ch, off).start()
 
-    def place(ch):
-        return ch if 2 * ch < chunks else chunks + chunks // 2 - 1 - ch
-
     def store_copies(ch):
-        lanes = pl.ds(place(ch) * CHUNK, CHUNK)
+        lanes = pl.ds((ch - 2) * CHUNK, CHUNK)
         return (
-            pltpu.make_async_copy(wide_high.at[ch], high_out.at[:, :, lanes], store_sem.at[ch, 0]),
-            pltpu.make_async_copy(wide_low.at[ch], low_out.at[:, :, lanes], store_sem.at[ch, 1]),
+            pltpu.make_async_copy(wide_high.at[ch], high_out.at[:, :, lanes], store_sem.at[ch - 2, 0]),
+            pltpu.make_async_copy(wide_low.at[ch], low_out.at[:, :, lanes], store_sem.at[ch - 2, 1]),
         )
+
+    def again(ch):
+        return pltpu.make_async_copy(field.at[:, :, pl.ds(ORDER[ch] * CHUNK, CHUNK)], u.at[ch], again_sem.at[ch])
+
+    def early_copy(x, slot):
+        return pltpu.make_async_copy(firsts.at[slot], early_out.at[x], early_sem.at[slot])
+
+    def early(start, stop):
+        def body(k, carry):
+            for slot in range(2):
+                x = 2 * k + slot
+
+                @pl.when(k > 0)
+                def _():
+                    early_copy(x - 2, slot).wait()
+
+                high = jnp.concatenate([wide_high[0, x], wide_high[1, x]], axis=1)
+                low = jnp.concatenate([wide_low[0, x], wide_low[1, x]], axis=1)
+                for at, part_rows in enumerate((high, low, high, low)):
+                    rhs[slot, at * modes : (at + 1) * modes, :] = part_rows
+                both = jnp.concatenate([u[0, x], u[1, x]], axis=1)
+                h = dot(jnp.concatenate([synth[...], both, both], axis=1), rhs[slot])
+                wide = both.astype(jnp.float32)
+                firsts[slot, :, :CHUNK] = wide[:, :CHUNK] + act(h[:, :CHUNK])
+                firsts[slot, :, CHUNK:] = turn(wide[:, CHUNK:], chans) + act(h[:, CHUNK:])
+                early_copy(x, slot).start()
+            return carry
+
+        lax.fori_loop(start // 2, stop // 2, body, 0)
 
     def expand(ch):
         for off in range(chips):
@@ -538,8 +575,9 @@
                 lanes = slice(at * CHUNK, (at + 1) * CHUNK)
                 wide_high[ch, :, take, :] = high[:, lanes].reshape(rows, 16, CHUNK)
                 wide_low[ch, :, take, :] = low[:, lanes].reshape(rows, 16, CHUNK)
-        for copy in store_copies(ch):
-            copy.start()
+        if ch >= 2:
+            for copy in store_copies(ch):
+                copy.start()
 
     analyse(0)
     pl.semaphore_wait(barrier, chips)
@@ -550,6 +588,8 @@
         pair_copy(ch).start()
         if ch > 1:
             emit(ch - 1)
+    again(0).start()
+    again(1).start()
     emit(chunks - 1)
     for copy in tables()[1:]:
         copy.wait()
@@ -558,11 +598,20 @@
         copy.start()
     for ch in range(chunks):
         blend(ch)
-    for ch in range(chunks):
-        hand(ch)
-        if ch >= 1:
-            expand(ch - 1)
-    expand(chunks - 1)
+    hand(0)
+    hand(1)
+    expand(0)
+    expand(1)
+    again(0).wait()
+    again(1).wait()
+    early(0, rows // 2)
+    hand(2)
+    early(rows // 2, rows)
+    hand(3)
+    expand(2)
+    expand(3)
+    for slot in range(2):
+        early_copy(rows - 2 + slot, slot).wait()
     for ch in range(chunks):
         pair_copy(ch).wait_send()
         for off in range(1, chips):
@@ -570,6 +619,7 @@
             in_copy(ch, off).wait_send()
         for off in range(chips):
             hand_copy(ch, off).wait_send()
+    for ch in range(2, chunks):
         for copy in store_copies(ch):
             copy.wait()
     for copy in ops_copies():
@@ -592,12 +642,13 @@
     return pl.pallas_call(
         functools.partial(exchange_kernel, chips, held, tall, chans),
         in_specs=[hbm] * 9 + [whole(a) for a in args[9:]],
-        out_specs=[hbm] * 4,
+        out_specs=[hbm] * 5,
         out_shape=[
-            jax.ShapeDtypeStruct((rows, modes, cells), bf16),
-            jax.ShapeDtypeStruct((rows, modes, cells), bf16),
+            jax.ShapeDtypeStruct((rows, modes, half), bf16),
+            jax.ShapeDtypeStruct((rows, modes, half), bf16),
             jax.ShapeDtypeStruct((2, 3 * half, half), bf16),
-            jax.ShapeDtypeStruct((2, 2 * half, half), bf16),
+            jax.ShapeDtypeStruct((2 * half, half), bf16),
+            jax.ShapeDtypeStruct((rows, width, half), f32),
         ],
         scratch_shapes=[
             pltpu.VMEM((2, rows, width, CHUNK), bf16),
@@ -613,7 +664,9 @@
             pltpu.VMEM((chunks, rows, modes, CHUNK), bf16),
             pltpu.VMEM((2 * chans - 1, size, 128), f32),
             pltpu.VMEM((2, 3 * half, half), bf16),
-            pltpu.VMEM((2, 2 * half, half), bf16),
+            pltpu.VMEM((2 * half, half), bf16),
+            pltpu.VMEM((2, width, half), f32),
+            pltpu.VMEM((2, 4 * modes + 2 * half, half), bf16),
             pltpu.VMEM(press_all.shape[1:], bf16),
             pltpu.VMEM(grow_all.shape[1:], bf16),
             *[pltpu.VMEM(a.shape, a.dtype) for a in args[3:9]],
@@ -627,14 +680,16 @@
             dma((chunks, chips - 1)),
             dma((chunks, chips)),
             dma((chunks, chips)),
-            dma((chunks, 2)),
+            dma((2, 2)),
+            dma((2,)),
+            dma((2,)),
             dma((2,)),
         ],
         compiler_params=pltpu.CompilerParams(collective_id=5, has_side_effects=True, vmem_limit_bytes=58 * MIB),
     )(*args)
 
 
-def finish_kernel(chans, u_ref, high_ref, low_ref, basis_ref, local_ref, depth_ref, out_ref, *rhs):
+def finish_kernel(chans, u_ref, high_ref, low_ref, early_ref, basis_ref, local_ref, depth_ref, out_ref, *rhs):
     rows, width, cells = u_ref.shape
     half = cells // 2
     modes = high_ref.shape[1]
@@ -642,20 +697,21 @@
     @pl.when(pl.program_id(0) == 0)
     def _():
         for r in rhs:
-            r[:, 4 * modes :, :] = local_ref[...]
+            r[4 * modes :, :] = local_ref[...]
 
     def first_layer(row):
         high, low = high_ref[row], low_ref[row]
-        parts = []
-        for side in range(2):
-            lanes = slice(side * half, (side + 1) * half)
-            for k, x in enumerate((high, low, high, low)):
-                rhs[row][side, modes * k : modes * (k + 1), :] = x[:, lanes]
-            u = u_ref[row, :, lanes]
-            h = dot(jnp.concatenate([basis_ref[...], u, u], axis=1), rhs[row][side])
-            wide = u.astype(jnp.float32)
-            parts.append((turn(wide, chans) if side else wide) + act(h))
-        return parts
+        for k, x in enumerate((high, low, high, low)):
+            rhs[row][modes * k : modes * (k + 1), :] = x
+        u = u_ref[row, :, CHUNK : CHUNK + half]
+        h = dot(jnp.concatenate([basis_ref[...], u, u], axis=1), rhs[row][...])
+        wide = u.astype(jnp.float32)
+        lower = wide[:, :CHUNK] + act(h[:, :CHUNK])
+        upper = turn(wide[:, CHUNK:], chans) + act(h[:, CHUNK:])
+        return [
+            jnp.concatenate([early_ref[row, :, :CHUNK], lower], axis=1),
+            jnp.concatenate([early_ref[row, :, CHUNK:], upper], axis=1),
+        ]
 
     def second_layer(row, first):
         mixes = []
@@ -673,27 +729,28 @@
         second_layer(row, firsts[row])
 
 
-def finish(field, high, low, basis, local, depth, chans):
+def finish(field, high, low, early, basis, local, depth, chans):
     rows, width, cells = field.shape
     modes = high.shape[1]
     step = math.gcd(rows, 2)
     whole = lambda a: pl.BlockSpec(a.shape, lambda i: (0,) * a.ndim)
     block = pl.BlockSpec((step, width, cells), lambda i: (i, 0, 0))
-    thin = pl.BlockSpec((step, modes, cells), lambda i: (i, 0, 0))
+    thin = pl.BlockSpec((step, modes, cells // 2), lambda i: (i, 0, 0))
+    wide = pl.BlockSpec((step, width, cells // 2), lambda i: (i, 0, 0))
     return pl.pallas_call(
         functools.partial(finish_kernel, chans),
         grid=(rows // step,),
-        in_specs=[block, thin, thin, whole(basis), whole(local), whole(depth)],
+        in_specs=[block, thin, thin, wide, whole(basis), whole(local), whole(depth)],
         out_specs=block,
         out_shape=jax.ShapeDtypeStruct(field.shape, jnp.bfloat16),
-        scratch_shapes=[pltpu.VMEM((2, 4 * modes + cells, cells // 2), jnp.bfloat16)] * step,
+        scratch_shapes=[pltpu.VMEM((4 * modes + cells, cells // 2), jnp.bfloat16)] * step,
         compiler_params=pltpu.CompilerParams(vmem_limit_bytes=56 * MIB),
         cost_estimate=pl.CostEstimate(
             flops=2 * rows * width * cells * (3 * cells),
             bytes_accessed=4 * rows * width * cells,
             transcendentals=2 * rows * width * cells,
         ),
-    )(field, high, low, basis, local, depth)
+    )(field, high, low, early, basis, local, depth)
 
 
 def stack_halves(x, order, axis):
@@ -756,9 +813,9 @@
     args = [field] + [jnp.asarray(a) for a in tables] + [jnp.asarray(front_y), lat_gains.T]
     args += [lat_modes.transpose(1, 2, 0).reshape(chans * chans, modes_x)]
     args += [jnp.asarray(a) for a in (spread8, spread16, spread16.T.copy())]
-    args += [depth_modes.reshape(modes_z * chans, chans), depth_local, lat_local]
-    high, low, depth_ops, local_ops = exchange(chips, held, tall, block, chans, *args)
-    return finish(field, high, low, jnp.asarray(back_y), local_ops, depth_ops, chans)
+    args += [depth_modes.reshape(modes_z * chans, chans), depth_local, lat_local, jnp.asarray(back_y)]
+    high, low, depth_ops, local_ops, early = exchange(chips, held, tall, block, chans, *args)
+    return finish(field, high, low, early, jnp.asarray(back_y), local_ops, depth_ops, chans)
 
 
 def lead_rows(held, rank):
@@ -782,7 +839,7 @@
     modes_y, modes_z = lat_gains.shape[0], depth_modes.shape[0]
     args = (field, lat_modes, lat_gains, lat_local, depth_modes, depth_local)
     fits = devices % 2 == 0 and modes_y % (2 * devices) == 0 and modes_y % 64 == 0 and 16 % (modes_y // devices) == 0
-    fits = fits and rows % 8 == 0 and cells % (4 * CHUNK) == 0 and chans * modes_z == 256 and cells == 512 and chans * chans == 256
+    fits = fits and rows % 8 == 0 and cells == 4 * CHUNK and chans * modes_z == 256 and cells == 512 and chans * chans == 256
     if fits:
         held = modes_y // devices
         factors = window_factors(wide_basis(rows * devices, modes_x), devices // 2, 1)

time: 99.6 us -> 110 us (1.10)
  Pallas kernels: 99.4 us -> 109 us
    pallas_call x1, Pallas kernels: 55.8 us -> 72.6 us  [exchange(): pl.pallas_call(functools.partial(exchange_kernel, chips, held, tall, chan...]
    pallas_call x1, Pallas kernels: 43.6 us -> 36.4 us  [finish(): pl.pallas_call(functools.partial(finish_kernel, chans), grid=(rows // ste...]
where the time goes in v4:
time: 110 us; the launch traced here: 109 us
  Pallas kernels  109 us (99%)
    pallas_call x1, Pallas kernels, exchange(): pl.pallas_call(functools.partial(exchange_kernel, chips, held, tall, chan...  72.6 us
    pallas_call x1, Pallas kernels, finish(): pl.pallas_call(functools.partial(finish_kernel, chans), grid=(rows // ste...  36.4 us

profile of v4, /device:TPU:0, one launch (start us, length us, event | category | flops | bytes accessed | tf_op | source)
XLA Modules:
  0.0 109.1 jit_solution(1864476773861632260)
XLA Ops:
  0.0 72.6 %shard_map.181 = (bf16[32,64,256]{2,1,0:T(8,128)(2,1)}, bf16[32,64,256]{2,1,0:T(8,128)(2,1)}, bf16[2,768,256]{2,1,0:T(8,128)(2,1)}, bf16[512,256]{1,0:T(8,128)(2,1)}, f32[32,512,256]{2,1,0:T(8,128)}) custom-call(bf16[32,512,512]{2,1,0:T(8,128)(2,1)} %u_ref.1, bf16[16,448,1536]{2,1,0:T(8,128)(2,1)} %constant.26.clone.refs_1_, ...), custom_call_target="tpu_custom_call" | custom-call | tf_op jit(solution)/shard_map/pallas_call | solution.py:642
  72.7 36.4 %shard_map.182 = bf16[32,512,512]{2,1,0:T(8,128)(2,1)} custom-call(bf16[32,512,512]{2,1,0:T(8,128)(2,1)} %u_ref.1, bf16[32,64,256]{2,1,0:T(8,128)(2,1)} %get-tuple-element.10.high_ref, bf16[32,64,256]{2,1,0:T(8,128)(2,1)} %get-tuple-element.11.low_ref, f32[32,512,256]{2,1,0:T(8,128)} %get-tuple-element.12.early_ref, ...), custom_call_target="tpu_custom_call" | custom-call | flops 25769803776 | bytes 33554432 | tf_op jit(solution)/shard_map/pallas_call | solution.py:740

commit v5 on v4

--- a/solution.py
+++ b/solution.py
@@ -304,6 +304,7 @@
 LEAD = 9
 CHUNK = 128
 ORDER = (0, 3, 1, 2)
+EARLY = 4
 
 
 def exact(a, b):
@@ -454,7 +455,7 @@
             out_copy(ch, off).start()
         land[ch, chip] = send[ch, chip]
 
-    def prepare():
+    def mixers():
         rest, total = modes_in[...], None
         for _ in range(3):
             term = rest.astype(jnp.bfloat16)
@@ -463,6 +464,8 @@
             total = product if total is None else total + product
         for at in range(2 * chans - 1):
             diags[at] = total[:, at * 128 : (at + 1) * 128]
+
+    def prepare():
         half = folds.shape[1]
         local = exact(exact(spread_t[...], depth_local[...]), spread16[...]) * block_mask(half, chans, False)
         for side in range(2):
@@ -475,7 +478,7 @@
         high, low = halves(spot * quarter_mask(half, chans))
         local_ops[:half, :] = high
         local_ops[half:, :] = low
-        for slot in range(2):
+        for slot in range(EARLY):
             rhs[slot, 4 * modes : 4 * modes + half, :] = high
             rhs[slot, 4 * modes + half :, :] = low
 
@@ -536,27 +539,33 @@
         return pltpu.make_async_copy(firsts.at[slot], early_out.at[x], early_sem.at[slot])
 
     def early(start, stop):
+        def draw(x, slot):
+            high = jnp.concatenate([wide_high[0, x], wide_high[1, x]], axis=1)
+            low = jnp.concatenate([wide_low[0, x], wide_low[1, x]], axis=1)
+            for at, part_rows in enumerate((high, low, high, low)):
+                rhs[slot, at * modes : (at + 1) * modes, :] = part_rows
+            both = jnp.concatenate([u[0, x], u[1, x]], axis=1)
+            return both, dot(jnp.concatenate([synth[...], both, both], axis=1), rhs[slot])
+
         def body(k, carry):
-            for slot in range(2):
-                x = 2 * k + slot
-
-                @pl.when(k > 0)
-                def _():
-                    early_copy(x - 2, slot).wait()
-
-                high = jnp.concatenate([wide_high[0, x], wide_high[1, x]], axis=1)
-                low = jnp.concatenate([wide_low[0, x], wide_low[1, x]], axis=1)
-                for at, part_rows in enumerate((high, low, high, low)):
-                    rhs[slot, at * modes : (at + 1) * modes, :] = part_rows
-                both = jnp.concatenate([u[0, x], u[1, x]], axis=1)
-                h = dot(jnp.concatenate([synth[...], both, both], axis=1), rhs[slot])
+            @pl.when(k > 0)
+            def _():
+                for slot in range(EARLY):
+                    early_copy(EARLY * (k - 1) + slot, slot).wait()
+
+            drawn = [draw(EARLY * k, 0)]
+            for slot in range(EARLY):
+                if slot + 1 < EARLY:
+                    drawn.append(draw(EARLY * k + slot + 1, slot + 1))
+                both, h = drawn[slot]
                 wide = both.astype(jnp.float32)
                 firsts[slot, :, :CHUNK] = wide[:, :CHUNK] + act(h[:, :CHUNK])
                 firsts[slot, :, CHUNK:] = turn(wide[:, CHUNK:], chans) + act(h[:, CHUNK:])
-                early_copy(x, slot).start()
+            for slot in range(EARLY):
+                early_copy(EARLY * k + slot, slot).start()
             return carry
 
-        lax.fori_loop(start // 2, stop // 2, body, 0)
+        lax.fori_loop(start // EARLY, stop // EARLY, body, 0)
 
     def expand(ch):
         for off in range(chips):
@@ -583,35 +592,44 @@
     pl.semaphore_wait(barrier, chips)
     pair_copy(0).start()
     emit(0)
-    for ch in range(1, chunks):
-        analyse(ch)
-        pair_copy(ch).start()
-        if ch > 1:
-            emit(ch - 1)
+    analyse(1)
+    pair_copy(1).start()
+    for copy in tables()[1:]:
+        copy.wait()
+    mixers()
+    emit(1)
+    analyse(2)
+    pair_copy(2).start()
+    blend(0)
+    analyse(3)
+    pair_copy(3).start()
     again(0).start()
     again(1).start()
-    emit(chunks - 1)
-    for copy in tables()[1:]:
-        copy.wait()
+    blend(1)
+    emit(2)
+    emit(3)
     prepare()
     for copy in ops_copies():
         copy.start()
-    for ch in range(chunks):
-        blend(ch)
     hand(0)
     hand(1)
     expand(0)
     expand(1)
     again(0).wait()
     again(1).wait()
-    early(0, rows // 2)
+    quarter = rows // 4
+    early(0, quarter)
+    blend(2)
+    early(quarter, 2 * quarter)
+    blend(3)
+    early(2 * quarter, 3 * quarter)
     hand(2)
-    early(rows // 2, rows)
+    early(3 * quarter, rows)
     hand(3)
     expand(2)
     expand(3)
-    for slot in range(2):
-        early_copy(rows - 2 + slot, slot).wait()
+    for slot in range(EARLY):
+        early_copy(rows - EARLY + slot, slot).wait()
     for ch in range(chunks):
         pair_copy(ch).wait_send()
         for off in range(1, chips):
@@ -665,8 +683,8 @@
             pltpu.VMEM((2 * chans - 1, size, 128), f32),
             pltpu.VMEM((2, 3 * half, half), bf16),
             pltpu.VMEM((2 * half, half), bf16),
-            pltpu.VMEM((2, width, half), f32),
-            pltpu.VMEM((2, 4 * modes + 2 * half, half), bf16),
+            pltpu.VMEM((EARLY, width, half), f32),
+            pltpu.VMEM((EARLY, 4 * modes + 2 * half, half), bf16),
             pltpu.VMEM(press_all.shape[1:], bf16),
             pltpu.VMEM(grow_all.shape[1:], bf16),
             *[pltpu.VMEM(a.shape, a.dtype) for a in args[3:9]],
@@ -683,7 +701,7 @@
             dma((2, 2)),
             dma((2,)),
             dma((2,)),
-            dma((2,)),
+            dma((EARLY,)),
         ],
         compiler_params=pltpu.CompilerParams(collective_id=5, has_side_effects=True, vmem_limit_bytes=58 * MIB),
     )(*args)
@@ -732,7 +750,7 @@
 def finish(field, high, low, early, basis, local, depth, chans):
     rows, width, cells = field.shape
     modes = high.shape[1]
-    step = math.gcd(rows, 2)
+    step = math.gcd(rows, 4)
     whole = lambda a: pl.BlockSpec(a.shape, lambda i: (0,) * a.ndim)
     block = pl.BlockSpec((step, width, cells), lambda i: (i, 0, 0))
     thin = pl.BlockSpec((step, modes, cells // 2), lambda i: (i, 0, 0))
@@ -839,7 +857,7 @@
     modes_y, modes_z = lat_gains.shape[0], depth_modes.shape[0]
     args = (field, lat_modes, lat_gains, lat_local, depth_modes, depth_local)
     fits = devices % 2 == 0 and modes_y % (2 * devices) == 0 and modes_y % 64 == 0 and 16 % (modes_y // devices) == 0
-    fits = fits and rows % 8 == 0 and cells == 4 * CHUNK and chans * modes_z == 256 and cells == 512 and chans * chans == 256
+    fits = fits and rows % (4 * EARLY) == 0 and cells == 4 * CHUNK and chans * modes_z == 256 and cells == 512 and chans * chans == 256
     if fits:
         held = modes_y // devices
         factors = window_factors(wide_basis(rows * devices, modes_x), devices // 2, 1)

time: 110 us -> 98.2 us (0.89)
  Pallas kernels: 109 us -> 96.3 us
    pallas_call x1, Pallas kernels: 72.6 us -> 60.9 us  [exchange(): pl.pallas_call(functools.partial(exchange_kernel, chips, held, tall, chan...]
where the time goes in v5:
time: 98.2 us; the launch traced here: 96.3 us
  Pallas kernels  96.3 us (98%)
    pallas_call x1, Pallas kernels, exchange(): pl.pallas_call(functools.partial(exchange_kernel, chips, held, tall, chan...  60.9 us
    pallas_call x1, Pallas kernels, finish(): pl.pallas_call(functools.partial(finish_kernel, chans), grid=(rows // ste...  35.4 us

profile of v5, /device:TPU:0, one launch (start us, length us, event | category | flops | bytes accessed | tf_op | source)
XLA Modules:
  0.0 96.3 jit_solution(18429656960002255860)
XLA Ops:
  0.0 60.9 %shard_map.181 = (bf16[32,64,256]{2,1,0:T(8,128)(2,1)}, bf16[32,64,256]{2,1,0:T(8,128)(2,1)}, bf16[2,768,256]{2,1,0:T(8,128)(2,1)}, bf16[512,256]{1,0:T(8,128)(2,1)}, f32[32,512,256]{2,1,0:T(8,128)}) custom-call(bf16[32,512,512]{2,1,0:T(8,128)(2,1)} %u_ref.1, bf16[16,448,1536]{2,1,0:T(8,128)(2,1)} %constant.26.clone.refs_1_, ...), custom_call_target="tpu_custom_call" | custom-call | tf_op jit(solution)/shard_map/pallas_call | solution.py:660
  60.9 35.4 %shard_map.182 = bf16[32,512,512]{2,1,0:T(8,128)(2,1)} custom-call(bf16[32,512,512]{2,1,0:T(8,128)(2,1)} %u_ref.1, bf16[32,64,256]{2,1,0:T(8,128)(2,1)} %get-tuple-element.10.high_ref, bf16[32,64,256]{2,1,0:T(8,128)(2,1)} %get-tuple-element.11.low_ref, f32[32,512,256]{2,1,0:T(8,128)} %get-tuple-element.12.early_ref, ...), custom_call_target="tpu_custom_call" | custom-call | flops 25769803776 | bytes 33554432 | tf_op jit(solution)/shard_map/pallas_call | solution.py:758
